TPU v7x, 32 devices: a whole 2x2x4 slice. The times are simulated.
32 devices in a mesh: gx: 4 (over y, core), gy: 2 (over x), gz: 4 (over z).
Axes of the slice: x: 2, y: 2, z: 4, core: 2. Of those that a mesh axis runs over, the one named last changes fastest.
Arguments:
- populations: float32 [19, 32, 32, 512], P(None, 'gx', 'gy', 'gz'), may hold values from 0 to 1, as said below
- solid_fraction: float32 [32, 32, 512], P('gx', 'gy', 'gz'), may hold values from 0 to 1
- intersection: int32 [32, 32, 512], P('gx', 'gy', 'gz'), may hold values from 0 to 256, as said below
- touch: int32 [4, 2, 4, 256], P('gx', 'gy', 'gz'), may hold values from 0 to 3455, as said below
- particles: float32 [4, 2, 4, 6, 128], P('gx', 'gy', 'gz'), may hold values from -8 to 8, as said below
- contacts: int32 [4, 2, 4, 12, 128], P('gx', 'gy', 'gz'), may hold values from 0 to 3456, as said below
- dest_code: int32 [4, 2, 4, 128], P('gx', 'gy', 'gz'), may hold values from 4 to 22, as said below
- dest_slot: int32 [4, 2, 4, 128], P('gx', 'gy', 'gz'), may hold values from 0 to 127, as said below
Outputs:
- populations_next: float32 [19, 32, 32, 512], P(None, 'gx', 'gy', 'gz')
- particles_next: float32 [4, 2, 4, 6, 128], P('gx', 'gy', 'gz')
Inputs may be any that keep to these rules, and one draw needn't show every extreme that they name: intersection = 256 marks a cell that no sphere covers; otherwise a touch slot of the cell's block. `touch`: entry o * 128 + s names slot s of the block at offset o of the 27 neighbouring blocks, offsets ordered with x slowest; the entries of one block are distinct and name every slot of the block itself. `contacts`: 3456 marks an empty entry. `dest_code`: a sphere stays (code 13) or moves one block along one axis (codes 4, 10, 12, 14, 16, 22), never out of the mesh; every slot of every block receives exactly one record. `dest_slot`: see dest_code. `populations`: every population is positive. `particles`: positions, in radii from the block centre, lie within the block's half widths; speeds lie within -1.5 to 1.5.
All inputs are finite; a program needn't handle non-finite values.
Results may differ from a plain program's by a relative error of at most 0.000076.
Values sent between devices are 32-bit elements; how exact they have to be, the bound alone decides.
No kernel may reach another device: no remote copies, remote signals or barrier semaphores. Data moves between devices by JAX's collectives and lax.ppermute only.
A program may use at most 128 MiB of HBM per device.

v0:
```python
import math

import jax
import jax.numpy as jnp
from jax import lax
from jax.sharding import PartitionSpec as P

R = 8


LATTICE = [
    (0, 0, 0),
    (1, 0, 0),
    (-1, 0, 0),
    (0, 1, 0),
    (0, -1, 0),
    (0, 0, 1),
    (0, 0, -1),
    (1, 1, 0),
    (-1, -1, 0),
    (1, -1, 0),
    (-1, 1, 0),
    (1, 0, 1),
    (-1, 0, -1),
    (1, 0, -1),
    (-1, 0, 1),
    (0, 1, 1),
    (0, -1, -1),
    (0, 1, -1),
    (0, -1, 1),
]
OPPOSITE = [0, 2, 1, 4, 3, 6, 5, 8, 7, 10, 9, 12, 11, 14, 13, 16, 15, 18, 17]
WEIGHTS = [1.0 / 3.0] + [1.0 / 18.0] * 6 + [1.0 / 36.0] * 12
RELAX_TIME = 0.8
SPEED_UNIT = 0.05
FORCE_SCALE = 0.1
CONTACT_GAIN = 1.0
GRAVITY_STEP = 0.1


def padded(shard, sides, width):
    for axis, dim in sides:
        peers, length = (lax.axis_size(axis), shard.shape[dim])
        up = [(i, (i + 1) % peers) for i in range(peers - 1)]
        down = [(j, i) for i, j in up]
        last = lax.slice_in_dim(shard, length - width, length, axis=dim)
        first = lax.slice_in_dim(shard, 0, width, axis=dim)
        before = lax.ppermute(last, axis, up)
        after = lax.ppermute(first, axis, down)
        shard = jnp.concatenate([before, shard, after], axis=dim)
    return shard


def equilibrium(density, velocity):
    square = velocity[0] * velocity[0] + velocity[1] * velocity[1] + velocity[2] * velocity[2]
    result = []
    for vector, weight in zip(LATTICE, WEIGHTS):
        projected = vector[0] * velocity[0] + vector[1] * velocity[1] + vector[2] * velocity[2]
        result.append(
            weight * density * (1.0 + 3.0 * projected + 4.5 * projected * projected - 1.5 * square)
        )
    return jnp.stack(result)


def collide(populations, solid_weight, solid_velocity):
    lattice_table = jnp.array(LATTICE, jnp.float32)
    density = jnp.sum(populations, axis=0)
    momentum = jnp.tensordot(lattice_table.T, populations, axes=1, precision=lax.Precision.HIGHEST)
    velocity = momentum / density
    fluid_eq = equilibrium(density, velocity)
    solid_eq = equilibrium(density, solid_velocity)
    mirrored = jnp.stack([populations[mirror_index] for mirror_index in OPPOSITE])
    fluid_mirror = jnp.stack([fluid_eq[mirror_index] for mirror_index in OPPOSITE])
    exchange_term = mirrored - populations + solid_eq - fluid_mirror
    relaxed = (
        populations
        - (1.0 - solid_weight) / RELAX_TIME * (populations - fluid_eq)
        + solid_weight * exchange_term
    )
    cell_force = -jnp.tensordot(
        lattice_table.T, solid_weight * exchange_term, axes=1, precision=lax.Precision.HIGHEST
    )
    return (relaxed, cell_force)


def block_offsets(entries, slots_each, span_x, span_y, span_z, radius):
    block_code = jnp.arange(entries, dtype=jnp.int32) // slots_each
    return jnp.stack(
        [
            (block_code // 9 - 1).astype(jnp.float32) * (span_x / radius),
            (block_code // 3 % 3 - 1).astype(jnp.float32) * (span_y / radius),
            (block_code % 3 - 1).astype(jnp.float32) * (span_z / radius),
        ]
    )


def fold_ends(blocks_out, widened):
    return blocks_out[1] + widened[0] + widened[3]


def deliver(blocks_out):
    folded_x = fold_ends(
        blocks_out, padded(jnp.stack([blocks_out[0], blocks_out[2]]), (("gx", 0),), 1)
    )
    folded_y = fold_ends(folded_x, padded(jnp.stack([folded_x[0], folded_x[2]]), (("gy", 0),), 1))
    return fold_ends(folded_y, padded(jnp.stack([folded_y[0], folded_y[2]]), (("gz", 0),), 1))


def touch_sums(cell_force, intersection, touches):
    count = intersection.size
    width = math.gcd(count, 16384)
    turns = count // width
    block_forces = jnp.moveaxis(cell_force.reshape(3, turns, width), 1, 0)
    block_slots = intersection.reshape(turns, width)
    labels = jnp.arange(touches + 1, dtype=jnp.int32)

    def add_block(running, block_pair):
        block_force, block_slot = block_pair
        onehot = (block_slot[None, :] == labels[:, None]).astype(jnp.float32)
        return (
            running + jnp.einsum("dc,kc->dk", block_force, onehot, precision=lax.Precision.HIGHEST),
            None,
        )

    running, unused = lax.scan(
        add_block, jnp.zeros((3, touches + 1), jnp.float32), (block_forces, block_slots)
    )
    return running[:, :touches]


def body(
    populations, solid_fraction, intersection, touch, particles, contacts, dest_code, dest_slot
):
    span_x, span_y, span_z = (populations.shape[1], populations.shape[2], populations.shape[3])
    particle_slots = particles.shape[4]
    touches = touch.shape[3]
    neighbours = contacts.shape[3]
    entries = 27 * particle_slots
    nearby = padded(particles, (("gx", 0), ("gy", 1), ("gz", 2)), 1)
    records_near = jnp.transpose(nearby.reshape(27, 6, particle_slots), (1, 0, 2)).reshape(
        6, entries
    )
    touch_rows = touch.reshape(touches)
    touch_velocity = jnp.concatenate(
        [jnp.take(records_near[3:6], touch_rows, axis=1), jnp.zeros((3, 1), jnp.float32)], axis=1
    )
    solid_velocity = SPEED_UNIT * jnp.take(touch_velocity, intersection, axis=1)
    solid_weight = jnp.where(
        intersection < touches,
        solid_fraction * (RELAX_TIME - 0.5) / (1.0 - solid_fraction + (RELAX_TIME - 0.5)),
        jnp.float32(0.0),
    )
    relaxed, cell_force = collide(populations, solid_weight, solid_velocity)
    widened = padded(relaxed, (("gx", 1), ("gy", 2), ("gz", 3)), 1)
    pulled = jnp.stack(
        [
            widened[
                direction,
                1 - vector[0] : 1 - vector[0] + span_x,
                1 - vector[1] : 1 - vector[1] + span_y,
                1 - vector[2] : 1 - vector[2] + span_z,
            ]
            for direction, vector in enumerate(LATTICE)
        ]
    )
    total_x = lax.axis_size("gx") * span_x
    total_y = lax.axis_size("gy") * span_y
    total_z = lax.axis_size("gz") * span_z
    coord_x = lax.axis_index("gx") * span_x + jnp.arange(span_x, dtype=jnp.int32)[:, None, None]
    coord_y = lax.axis_index("gy") * span_y + jnp.arange(span_y, dtype=jnp.int32)[None, :, None]
    coord_z = lax.axis_index("gz") * span_z + jnp.arange(span_z, dtype=jnp.int32)[None, None, :]
    passed = []
    for direction, vector in enumerate(LATTICE):
        inside = (
            (coord_x - vector[0] >= 0)
            & (coord_x - vector[0] < total_x)
            & (coord_y - vector[1] >= 0)
            & (coord_y - vector[1] < total_y)
            & (coord_z - vector[2] >= 0)
            & (coord_z - vector[2] < total_z)
        )
        passed.append(jnp.where(inside, pulled[direction], relaxed[OPPOSITE[direction]]))
    populations_next = jnp.stack(passed)
    touch_force = touch_sums(cell_force, intersection, touches)
    entry_ids = jnp.arange(entries, dtype=jnp.int32)
    picking = (touch_rows[:, None] == entry_ids[None, :]).astype(jnp.float32)
    spread = jnp.dot(touch_force, picking, precision=lax.Precision.HIGHEST)
    force_blocks = jnp.transpose(spread.reshape(3, 27, particle_slots), (1, 0, 2)).reshape(
        3, 3, 3, 3, particle_slots
    )
    hydro = deliver(force_blocks)
    offsets = block_offsets(entries + 1, particle_slots, span_x, span_y, span_z, R)
    partner_table = (
        jnp.concatenate([records_near[0:3], jnp.zeros((3, 1), jnp.float32)], axis=1) + offsets
    )
    contact_rows = contacts.reshape(neighbours, particle_slots)
    partner = jnp.take(partner_table, contact_rows, axis=1)
    own_records = particles.reshape(6, particle_slots)
    separation = own_records[0:3, None, :] - partner
    valid = (contact_rows < entries).astype(jnp.float32)
    square = jnp.sum(separation * separation, axis=0)
    soften = 1.0 + 0.25 * square
    strength = CONTACT_GAIN * valid / (soften * soften)
    contact_force = jnp.sum(separation * strength[None], axis=1)
    gravity = jnp.array([0.0, 0.0, GRAVITY_STEP], jnp.float32)
    velocity_new = own_records[3:6] + FORCE_SCALE * hydro + contact_force - gravity[:, None]
    position_new = own_records[0:3] + velocity_new * (SPEED_UNIT / R)
    dest_codes = dest_code.reshape(particle_slots)
    code_ids = jnp.arange(27, dtype=jnp.int32)
    routing = (dest_codes[None, :] == code_ids[:, None]).astype(jnp.float32)
    placing = (
        dest_slot.reshape(particle_slots)[:, None]
        == jnp.arange(particle_slots, dtype=jnp.int32)[None, :]
    ).astype(jnp.float32)
    code_shift = block_offsets(27, 1, span_x, span_y, span_z, R)
    moved_position = position_new[None] - code_shift.T[:, :, None]
    candidates = jnp.concatenate(
        [moved_position, jnp.broadcast_to(velocity_new[None], (27, 3, particle_slots))], axis=1
    )
    candidates = candidates * routing[:, None, :]
    record_blocks = jnp.einsum("cwp,pt->cwt", candidates, placing, precision=lax.Precision.HIGHEST)
    arrived = deliver(record_blocks.reshape(3, 3, 3, 6, particle_slots))
    return (populations_next, arrived.reshape(1, 1, 1, 6, particle_slots))


def solution(mesh):
    placed = (
        P(None, "gx", "gy", "gz"),
        P("gx", "gy", "gz"),
        P("gx", "gy", "gz"),
        P("gx", "gy", "gz", None),
        P("gx", "gy", "gz", None, None),
        P("gx", "gy", "gz", None, None),
        P("gx", "gy", "gz", None),
        P("gx", "gy", "gz", None),
    )
    return jax.shard_map(
        body,
        mesh=mesh,
        in_specs=placed,
        out_specs=(P(None, "gx", "gy", "gz"), P("gx", "gy", "gz", None, None)),
        check_vma=False,
    )
```

profile of v0, /device:TPU:0, one launch (start us, length us, event | category | flops | bytes accessed | tf_op | source)
XLA Modules:
  0.0 233.3 jit_solution(8805699256080424560)
XLA Ops:
  0.7 2.5 %collective-permute-start = (f32[1,1,1,6,128]{4,2,3,1,0:T(1,128)}, f32[1,1,1,6,128]{4,2,3,1,0:T(1,128)S(1)}, u32[]{:S(2)}, u32[]{:S(2)}) collective-permute-start(f32[1,1,1,6,128]{4,2,3,1,0:T(1,128)} %param.14), channel_id=1, source_target_pairs={{0,8},{8,16},{16,24},{1,9},{9,17},{17,25},{2,10},{10,18},{18,26},{... | collective-permute-start | bytes 9224 | tf_op jit(solution)/shard_map/ppermute | solution.py:48
  19.6 4.2 %collective-permute-start.2 = (f32[3,1,1,6,128]{4,2,3,1,0:T(1,128)S(1)}, f32[3,1,1,6,128]{4,2,3,1,0:T(1,128)S(1)}, u32[]{:S(2)}, u32[]{:S(2)}) collective-permute-start(f32[3,1,1,6,128]{4,2,3,1,0:T(1,128)S(1)} %constant_dynamic-update-slice_fusion.38), channel_id=1, source_target_pairs={{0,4},{1,5},{2,6},{3,7},{8,12},{9,13},{10,14},{11,15},{16,20},{17,... | collective-permute-start | bytes 27656 | tf_op jit(solution)/shard_map/ppermute | solution.py:48
  25.7 3.6 %collective-permute-done.3 = f32[3,1,1,6,128]{4,2,3,1,0:T(1,128)S(1)} collective-permute-done((f32[3,1,1,6,128]{4,2,3,1,0:T(1,128)S(1)}, f32[3,1,1,6,128]{4,2,3,1,0:T(1,128)S(1)}, u32[]{:S(2)}, u32[]{:S(2)}) %collective-permute-start.3) | collective-permute-done | bytes 9248 | tf_op jit(solution)/shard_map/ppermute | solution.py:49
  29.4 3.5 %collective-permute-start.4 = (f32[3,3,1,6,128]{4,2,3,1,0:T(1,128)S(1)}, f32[3,3,1,6,128]{4,2,3,1,0:T(1,128)S(1)}, u32[]{:S(2)}, u32[]{:S(2)}) collective-permute-start(f32[3,3,1,6,128]{4,2,3,1,0:T(1,128)S(1)} %pad_maximum_fusion.24), channel_id=1, source_target_pairs={{0,1},{1,2},{2,3},{4,5},{5,6},{6,7},{8,9},{9,10},{10,11},{12,13},{... | collective-permute-start | bytes 82952 | tf_op jit(solution)/shard_map/ppermute | solution.py:48
  34.7 1.8 copy.191
  43.3 60.2 %gather_fusion.1 = f32[16384,3]{1,0:T(8,128)} fusion(f32[3,257]{0,1:T(8,128)S(1)} %concatenate.58, s32[16384]{0:T(1024)} %broadcast_clamp_fusion), kind=kCustom, calls=%fused_computation.1 | custom fusion | bytes 458752 | tf_op jit(solution)/shard_map/jit(_take)/gather | solution.py:147
  103.5 5.2 %copy.199 = f32[8,16,128,3]{2,1,0,3:T(8,128)S(1)} copy(f32[8,16,128,3]{3,2,1,0:T(8,128)} %bitcast.178) | data formatting | bytes 393216 | tf_op jit(solution)/shard_map/jit(_take)/gather | solution.py:147
  112.2 1.8 fusion.9
  114.0 7.4 %fusion = f32[3,256]{1,0:T(4,128)S(1)} fusion(f32[3,16384]{1,0:T(4,128)S(1)} %bitcast.189, s32[16384]{0:T(1024)S(1)} %bitcast.185), kind=kOutput, calls=%fused_computation.4 | convolution fusion | flops 159383552 | bytes 265216 | tf_op jit(solution)/shard_map/while/body/eval_jaxpr/dc,kc->dk/dot_general | solution.py:121
  122.8 1.8 collective-permute-start.12
  125.9 1.8 copy.190
  127.7 3.4 %pad_add_fusion = f32[3,3457]{0,1:T(8,128)} fusion(f32[3,3457]{0,1:T(8,128)} %copy.191, f32[3,3456]{0,1:T(8,128)} %bitcast.179), kind=kLoop, calls=%fused_computation.10 | loop fusion | flops 10371 | bytes 124440 | tf_op jit(solution)/shard_map/add | solution.py:194
  131.1 4.1 %gather_fusion.2 = f32[1536,3]{1,0:T(8,128)S(1)} fusion(f32[3,3457]{0,1:T(8,128)} %pad_add_fusion, s32[2048]{0:T(1024)S(1)} %copy-done.13), kind=kCustom, calls=%fused_computation.2 | custom fusion | bytes 43008 | tf_op jit(solution)/shard_map/jit(_take)/gather | solution.py:197
  139.6 2.1 collective-permute-start.14
  143.0 1.8 collective-permute-done.14
  144.8 4.4 %collective-permute-done.15 = f32[1,3,3,128]{2,3,1,0:T(8,128)S(1)} collective-permute-done((f32[1,3,3,128]{2,3,1,0:T(8,128)S(1)}, f32[1,3,3,128]{2,3,1,0:T(8,128)S(1)}, u32[]{:S(2)}, u32[]{:S(2)}) %collective-permute-start.15) | collective-permute-done | bytes 4640 | tf_op jit(solution)/shard_map/ppermute | solution.py:49
  149.3 3.7 %collective-permute-start.16 = (f32[1,3,128]{1,2,0:T(8,128)S(1)}, f32[1,3,128]{1,2,0:T(8,128)S(1)}, u32[]{:S(2)}, u32[]{:S(2)}) collective-permute-start(f32[1,3,128]{1,2,0:T(8,128)S(1)} %get-tuple-element.81), channel_id=1, source_target_pairs={{0,1},{1,2},{2,3},{4,5},{5,6},{6,7},{8,9},{9,10},{10,11},{12,13},{... | collective-permute-start | bytes 4616 | tf_op jit(solution)/shard_map/ppermute | solution.py:48
  154.9 4.3 %collective-permute-done.17 = f32[1,3,128]{1,2,0:T(8,128)S(1)} collective-permute-done((f32[1,3,128]{1,2,0:T(8,128)S(1)}, f32[1,3,128]{1,2,0:T(8,128)S(1)}, u32[]{:S(2)}, u32[]{:S(2)}) %collective-permute-start.17) | collective-permute-done | bytes 1568 | tf_op jit(solution)/shard_map/ppermute | solution.py:49
  159.8 3.3 %collective-permute-start.18 = (f32[1,3,3,6,128]{4,3,2,1,0:T(8,128)S(1)}, f32[1,3,3,6,128]{4,3,2,1,0:T(8,128)S(1)}, u32[]{:S(2)}, u32[]{:S(2)}) collective-permute-start(f32[1,3,3,6,128]{4,3,2,1,0:T(8,128)S(1)} %bitcast.194), channel_id=1, source_target_pairs={{0,8},{8,16},{16,24},{1,9},{9,17},{17,25},{2,10},{10,18},{18,26},{... | collective-permute-start | bytes 82952 | tf_op jit(solution)/shard_map/ppermute | solution.py:48
  164.4 5.9 %collective-permute-done.19 = f32[1,3,3,6,128]{4,3,2,1,0:T(8,128)S(1)} collective-permute-done((f32[1,3,3,6,128]{4,3,2,1,0:T(8,128)S(1)}, f32[1,3,3,6,128]{4,3,2,1,0:T(8,128)S(1)}, u32[]{:S(2)}, u32[]{:S(2)}) %collective-permute-start.19) | collective-permute-done | bytes 27680 | tf_op jit(solution)/shard_map/ppermute | solution.py:49
  173.2 4.2 %collective-permute-done.21 = f32[1,3,6,128]{3,2,1,0:T(8,128)S(1)} collective-permute-done((f32[1,3,6,128]{3,2,1,0:T(8,128)S(1)}, f32[1,3,6,128]{3,2,1,0:T(8,128)S(1)}, u32[]{:S(2)}, u32[]{:S(2)}) %collective-permute-start.21) | collective-permute-done | bytes 9248 | tf_op jit(solution)/shard_map/ppermute | solution.py:49
  177.4 3.5 %collective-permute-start.22 = (f32[1,6,128]{2,1,0:T(8,128)S(1)}, f32[1,6,128]{2,1,0:T(8,128)S(1)}, u32[]{:S(2)}, u32[]{:S(2)}) collective-permute-start(f32[1,6,128]{2,1,0:T(8,128)S(1)} %get-tuple-element.111), channel_id=1, source_target_pairs={{0,1},{1,2},{2,3},{4,5},{5,6},{6,7},{8,9},{9,10},{10,11},{12,13},{... | collective-permute-start | bytes 9224 | tf_op jit(solution)/shard_map/ppermute | solution.py:48
  182.8 3.0 %collective-permute-start.6 = (f32[19,1,16,128]{3,2,1,0:T(8,128)S(1)}, f32[19,1,16,128]{3,2,1,0:T(8,128)S(1)}, u32[]{:S(2)}, u32[]{:S(2)}) collective-permute-start(f32[19,1,16,128]{3,2,1,0:T(8,128)S(1)} %get-tuple-element.78), channel_id=1, source_target_pairs={{0,8},{8,16},{16,24},{1,9},{9,17},{17,25},{2,10},{10,18},{18,26},{... | collective-permute-start | bytes 466952 | tf_op jit(solution)/shard_map/ppermute | solution.py:48
  187.7 2.4 %collective-permute-done.7 = f32[19,1,16,128]{3,2,1,0:T(8,128)S(1)} collective-permute-done((f32[19,1,16,128]{3,2,1,0:T(8,128)S(1)}, f32[19,1,16,128]{3,2,1,0:T(8,128)S(1)}, u32[]{:S(2)}, u32[]{:S(2)}) %collective-permute-start.7) | collective-permute-done | bytes 155680 | tf_op jit(solution)/shard_map/ppermute | solution.py:49
  194.7 3.7 %collective-permute-done.9 = f32[19,10,1,128]{3,2,1,0:T(1,128)S(1)} collective-permute-done((f32[19,10,1,128]{3,2,1,0:T(1,128)S(1)}, f32[19,10,1,128]{3,2,1,0:T(1,128)S(1)}, u32[]{:S(2)}, u32[]{:S(2)}) %collective-permute-start.9) | collective-permute-done | bytes 97312 | tf_op jit(solution)/shard_map/ppermute | solution.py:49
  198.8 2.9 %fusion.200 = (f32[19,10,18,1]{3,2,1,0:T(8,128)}, f32[19,10,18,1]{3,2,1,0:T(8,128)}) fusion(f32[19,10,18,128]{3,2,1,0:T(8,128)S(1)} %pad_maximum_fusion), kind=kLoop, calls=%fused_computation.451 | loop fusion | bytes 54720 | tf_op jit(solution)/shard_map/slice | solution.py:47
  201.7 2.8 %copy.177 = f32[19,10,18,1]{0,3,2,1:T(1,128)S(1)} copy(f32[19,10,18,1]{3,2,1,0:T(8,128)} %get-tuple-element.74) | data formatting | bytes 27360 | tf_op jit(solution)/shard_map/slice | solution.py:46
  204.5 4.7 %collective-permute-start.10 = (f32[19,10,18,1]{0,3,2,1:T(1,128)S(1)}, f32[19,10,18,1]{0,3,2,1:T(1,128)S(1)}, u32[]{:S(2)}, u32[]{:S(2)}) collective-permute-start(f32[19,10,18,1]{0,3,2,1:T(1,128)S(1)} %copy.177), channel_id=1, source_target_pairs={{0,1},{1,2},{2,3},{4,5},{5,6},{6,7},{8,9},{9,10},{10,11},{12,13},{... | collective-permute-start | bytes 41048 | tf_op jit(solution)/shard_map/ppermute | solution.py:48
  209.1 2.8 %copy.179 = f32[19,10,18,1]{0,3,2,1:T(1,128)S(1)} copy(f32[19,10,18,1]{3,2,1,0:T(8,128)} %get-tuple-element.73) | data formatting | bytes 27360 | tf_op jit(solution)/shard_map/slice | solution.py:47
  214.8 3.0 %copy.178 = f32[19,10,18,1]{3,2,1,0:T(8,128)} copy(f32[19,10,18,1]{0,3,2,1:T(1,128)S(1)} %collective-permute-done.10) | data formatting | bytes 27360 | tf_op jit(solution)/shard_map/ppermute | solution.py:48
  218.5 3.1 %copy.180 = f32[19,10,18,1]{3,2,1,0:T(8,128)} copy(f32[19,10,18,1]{0,3,2,1:T(1,128)S(1)} %collective-permute-done.11) | data formatting | bytes 27360 | tf_op jit(solution)/shard_map/ppermute | solution.py:49
  221.6 1.8 constant_dynamic-update-slice_fusion.92
  (252 shorter events, 66.9 us)
Async XLA Ops:
  0.7 18.9 %collective-permute-start = (f32[1,1,1,6,128]{4,2,3,1,0:T(1,128)}, f32[1,1,1,6,128]{4,2,3,1,0:T(1,128)S(1)}, u32[]{:S(2)}, u32[]{:S(2)}) collective-permute-start(f32[1,1,1,6,128]{4,2,3,1,0:T(1,128)} %param.14), channel_id=1, source_target_pairs={{0,8},{8,16},{16,24},{1,9},{9,17},{17,25},{2,10},{10,18},{18,26},{... | collective-permute-start | bytes 9224 | tf_op jit(solution)/shard_map/ppermute | solution.py:48
  3.2 16.3 %collective-permute-start.1 = (f32[1,1,1,6,128]{4,2,3,1,0:T(1,128)}, f32[1,1,1,6,128]{4,2,3,1,0:T(1,128)S(1)}, u32[]{:S(2)}, u32[]{:S(2)}) collective-permute-start(f32[1,1,1,6,128]{4,2,3,1,0:T(1,128)} %param.14), channel_id=1, source_target_pairs={{8,0},{16,8},{24,16},{9,1},{17,9},{25,17},{10,2},{18,10},{26,18},{... | collective-permute-start | bytes 9224 | tf_op jit(solution)/shard_map/ppermute | solution.py:49
  19.6 6.1 %collective-permute-start.2 = (f32[3,1,1,6,128]{4,2,3,1,0:T(1,128)S(1)}, f32[3,1,1,6,128]{4,2,3,1,0:T(1,128)S(1)}, u32[]{:S(2)}, u32[]{:S(2)}) collective-permute-start(f32[3,1,1,6,128]{4,2,3,1,0:T(1,128)S(1)} %constant_dynamic-update-slice_fusion.38), channel_id=1, source_target_pairs={{0,4},{1,5},{2,6},{3,7},{8,12},{9,13},{10,14},{11,15},{16,20},{17,... | collective-permute-start | bytes 27656 | tf_op jit(solution)/shard_map/ppermute | solution.py:48
  23.8 5.6 %collective-permute-start.3 = (f32[3,1,1,6,128]{4,2,3,1,0:T(1,128)S(1)}, f32[3,1,1,6,128]{4,2,3,1,0:T(1,128)S(1)}, u32[]{:S(2)}, u32[]{:S(2)}) collective-permute-start(f32[3,1,1,6,128]{4,2,3,1,0:T(1,128)S(1)} %constant_dynamic-update-slice_fusion.38), channel_id=1, source_target_pairs={{4,0},{5,1},{6,2},{7,3},{12,8},{13,9},{14,10},{15,11},{20,16},{21,... | collective-permute-start | bytes 27656 | tf_op jit(solution)/shard_map/ppermute | solution.py:49
  29.4 8.0 %collective-permute-start.4 = (f32[3,3,1,6,128]{4,2,3,1,0:T(1,128)S(1)}, f32[3,3,1,6,128]{4,2,3,1,0:T(1,128)S(1)}, u32[]{:S(2)}, u32[]{:S(2)}) collective-permute-start(f32[3,3,1,6,128]{4,2,3,1,0:T(1,128)S(1)} %pad_maximum_fusion.24), channel_id=1, source_target_pairs={{0,1},{1,2},{2,3},{4,5},{5,6},{6,7},{8,9},{9,10},{10,11},{12,13},{... | collective-permute-start | bytes 82952 | tf_op jit(solution)/shard_map/ppermute | solution.py:48
  32.8 5.8 %collective-permute-start.5 = (f32[3,3,1,6,128]{4,2,3,1,0:T(1,128)S(1)}, f32[3,3,1,6,128]{4,2,3,1,0:T(1,128)S(1)}, u32[]{:S(2)}, u32[]{:S(2)}) collective-permute-start(f32[3,3,1,6,128]{4,2,3,1,0:T(1,128)S(1)} %pad_maximum_fusion.24), channel_id=1, source_target_pairs={{1,0},{2,1},{3,2},{5,4},{6,5},{7,6},{9,8},{10,9},{11,10},{13,12},{... | collective-permute-start | bytes 82952 | tf_op jit(solution)/shard_map/ppermute | solution.py:49
  122.8 13.2 %collective-permute-start.12 = (f32[1,3,3,3,128]{4,0,3,2,1:T(1,128)S(1)}, f32[1,3,3,3,128]{4,0,3,2,1:T(1,128)S(1)}, u32[]{:S(2)}, u32[]{:S(2)}) collective-permute-start(f32[1,3,3,3,128]{4,0,3,2,1:T(1,128)S(1)} %copy.185), channel_id=1, source_target_pairs={{0,8},{8,16},{16,24},{1,9},{9,17},{17,25},{2,10},{10,18},{18,26},{... | collective-permute-start | bytes 41480 | tf_op jit(solution)/shard_map/ppermute | solution.py:48
  124.6 12.5 %collective-permute-start.13 = (f32[1,3,3,3,128]{4,0,3,2,1:T(1,128)S(1)}, f32[1,3,3,3,128]{4,0,3,2,1:T(1,128)S(1)}, u32[]{:S(2)}, u32[]{:S(2)}) collective-permute-start(f32[1,3,3,3,128]{4,0,3,2,1:T(1,128)S(1)} %copy.188), channel_id=1, source_target_pairs={{8,0},{16,8},{24,16},{9,1},{17,9},{25,17},{10,2},{18,10},{26,18},{... | collective-permute-start | bytes 41480 | tf_op jit(solution)/shard_map/ppermute | solution.py:49
  139.5 19.6 %copy-start.6 = (f32[1,1,1,3,128]{3,4,2,1,0:T(8,128)S(1)}, f32[1,1,1,3,128]{3,4,2,1,0:T(8,128)}, u32[]{:S(2)}) copy-start(f32[1,1,1,3,128]{3,4,2,1,0:T(8,128)} %copy.202) | copy-start | bytes 4612
  139.5 19.6 %copy-start.32 = (f32[3]{0:T(128)S(1)}, f32[3]{0:T(128)}, u32[]{:S(2)}) copy-start(f32[3]{0:T(128)} %constant.232) | copy-start | bytes 40
  139.6 5.3 %collective-permute-start.14 = (f32[1,3,3,128]{2,3,1,0:T(8,128)S(1)}, f32[1,3,3,128]{2,3,1,0:T(8,128)S(1)}, u32[]{:S(2)}, u32[]{:S(2)}) collective-permute-start(f32[1,3,3,128]{2,3,1,0:T(8,128)S(1)} %get-tuple-element.79), channel_id=1, source_target_pairs={{0,4},{1,5},{2,6},{3,7},{8,12},{9,13},{10,14},{11,15},{16,20},{17,... | collective-permute-start | bytes 13832 | tf_op jit(solution)/shard_map/ppermute | solution.py:48
  141.7 7.6 %collective-permute-start.15 = (f32[1,3,3,128]{2,3,1,0:T(8,128)S(1)}, f32[1,3,3,128]{2,3,1,0:T(8,128)S(1)}, u32[]{:S(2)}, u32[]{:S(2)}) collective-permute-start(f32[1,3,3,128]{2,3,1,0:T(8,128)S(1)} %get-tuple-element.80), channel_id=1, source_target_pairs={{4,0},{5,1},{6,2},{7,3},{12,8},{13,9},{14,10},{15,11},{20,16},{21,... | collective-permute-start | bytes 13832 | tf_op jit(solution)/shard_map/ppermute | solution.py:49
  143.0 16.3 %copy-start.23 = (f32[27,3]{0,1:T(4,128)S(1)}, f32[27,3]{0,1:T(4,128)}, u32[]{:S(2)}) copy-start(f32[27,3]{0,1:T(4,128)} %maximum_bitcast_fusion) | copy-start | bytes 976
  143.0 16.4 %copy-start.9 = (f32[27,128]{1,0:T(8,128)S(1)}, f32[27,128]{1,0:T(8,128)}, u32[]{:S(2)}) copy-start(f32[27,128]{1,0:T(8,128)} %fusion.143) | copy-start | bytes 41476
  143.0 16.4 %copy-start.31 = (s32[1,1,1,128]{3,2,1,0:T(1,128)S(1)}, s32[1,1,1,128]{3,2,1,0:T(1,128)}, u32[]{:S(2)}) copy-start(s32[1,1,1,128]{3,2,1,0:T(1,128)} %param.17) | copy-start | bytes 1540
  149.3 5.6 %collective-permute-start.16 = (f32[1,3,128]{1,2,0:T(8,128)S(1)}, f32[1,3,128]{1,2,0:T(8,128)S(1)}, u32[]{:S(2)}, u32[]{:S(2)}) collective-permute-start(f32[1,3,128]{1,2,0:T(8,128)S(1)} %get-tuple-element.81), channel_id=1, source_target_pairs={{0,1},{1,2},{2,3},{4,5},{5,6},{6,7},{8,9},{9,10},{10,11},{12,13},{... | collective-permute-start | bytes 4616 | tf_op jit(solution)/shard_map/ppermute | solution.py:48
  153.0 6.2 %collective-permute-start.17 = (f32[1,3,128]{1,2,0:T(8,128)S(1)}, f32[1,3,128]{1,2,0:T(8,128)S(1)}, u32[]{:S(2)}, u32[]{:S(2)}) collective-permute-start(f32[1,3,128]{1,2,0:T(8,128)S(1)} %get-tuple-element.82), channel_id=1, source_target_pairs={{1,0},{2,1},{3,2},{5,4},{6,5},{7,6},{9,8},{10,9},{11,10},{13,12},{... | collective-permute-start | bytes 4616 | tf_op jit(solution)/shard_map/ppermute | solution.py:49
  159.8 4.6 %collective-permute-start.18 = (f32[1,3,3,6,128]{4,3,2,1,0:T(8,128)S(1)}, f32[1,3,3,6,128]{4,3,2,1,0:T(8,128)S(1)}, u32[]{:S(2)}, u32[]{:S(2)}) collective-permute-start(f32[1,3,3,6,128]{4,3,2,1,0:T(8,128)S(1)} %bitcast.194), channel_id=1, source_target_pairs={{0,8},{8,16},{16,24},{1,9},{9,17},{17,25},{2,10},{10,18},{18,26},{... | collective-permute-start | bytes 82952 | tf_op jit(solution)/shard_map/ppermute | solution.py:48
  163.1 7.2 %collective-permute-start.19 = (f32[1,3,3,6,128]{4,3,2,1,0:T(8,128)S(1)}, f32[1,3,3,6,128]{4,3,2,1,0:T(8,128)S(1)}, u32[]{:S(2)}, u32[]{:S(2)}) collective-permute-start(f32[1,3,3,6,128]{4,3,2,1,0:T(8,128)S(1)} %bitcast.195), channel_id=1, source_target_pairs={{8,0},{16,8},{24,16},{9,1},{17,9},{25,17},{10,2},{18,10},{26,18},{... | collective-permute-start | bytes 82952 | tf_op jit(solution)/shard_map/ppermute | solution.py:49
  170.3 2.8 %collective-permute-start.20 = (f32[1,3,6,128]{3,2,1,0:T(8,128)S(1)}, f32[1,3,6,128]{3,2,1,0:T(8,128)S(1)}, u32[]{:S(2)}, u32[]{:S(2)}) collective-permute-start(f32[1,3,6,128]{3,2,1,0:T(8,128)S(1)} %get-tuple-element.109), channel_id=1, source_target_pairs={{0,4},{1,5},{2,6},{3,7},{8,12},{9,13},{10,14},{11,15},{16,20},{17,... | collective-permute-start | bytes 27656 | tf_op jit(solution)/shard_map/ppermute | solution.py:48
  171.8 5.6 %collective-permute-start.21 = (f32[1,3,6,128]{3,2,1,0:T(8,128)S(1)}, f32[1,3,6,128]{3,2,1,0:T(8,128)S(1)}, u32[]{:S(2)}, u32[]{:S(2)}) collective-permute-start(f32[1,3,6,128]{3,2,1,0:T(8,128)S(1)} %get-tuple-element.110), channel_id=1, source_target_pairs={{4,0},{5,1},{6,2},{7,3},{12,8},{13,9},{14,10},{15,11},{20,16},{21,... | collective-permute-start | bytes 27656 | tf_op jit(solution)/shard_map/ppermute | solution.py:49
  173.1 20.2 %copy-start.11 = (pred[128]{0:T(512)(128)(4,1)S(1)}, pred[128]{0:T(512)(128)(4,1)}, u32[]{:S(2)}) copy-start(pred[128]{0:T(512)(128)(4,1)} %get-tuple-element.134) | copy-start | bytes 388
  173.1 20.2 %copy-start.12 = (pred[128]{0:T(512)(128)(4,1)S(1)}, pred[128]{0:T(512)(128)(4,1)}, u32[]{:S(2)}) copy-start(pred[128]{0:T(512)(128)(4,1)} %get-tuple-element.135) | copy-start | bytes 388
  173.1 20.2 %copy-start.18 = (pred[8,16]{1,0:T(8,128)(4,1)S(1)}, pred[8,16]{1,0:T(8,128)(4,1)}, u32[]{:S(2)}) copy-start(pred[8,16]{1,0:T(8,128)(4,1)} %get-tuple-element.126) | copy-start | bytes 388
  177.4 9.7 %collective-permute-start.22 = (f32[1,6,128]{2,1,0:T(8,128)S(1)}, f32[1,6,128]{2,1,0:T(8,128)S(1)}, u32[]{:S(2)}, u32[]{:S(2)}) collective-permute-start(f32[1,6,128]{2,1,0:T(8,128)S(1)} %get-tuple-element.111), channel_id=1, source_target_pairs={{0,1},{1,2},{2,3},{4,5},{5,6},{6,7},{8,9},{9,10},{10,11},{12,13},{... | collective-permute-start | bytes 9224 | tf_op jit(solution)/shard_map/ppermute | solution.py:48
  180.9 6.2 %collective-permute-start.23 = (f32[1,6,128]{2,1,0:T(8,128)S(1)}, f32[1,6,128]{2,1,0:T(8,128)S(1)}, u32[]{:S(2)}, u32[]{:S(2)}) collective-permute-start(f32[1,6,128]{2,1,0:T(8,128)S(1)} %get-tuple-element.112), channel_id=1, source_target_pairs={{1,0},{2,1},{3,2},{5,4},{6,5},{7,6},{9,8},{10,9},{11,10},{13,12},{... | collective-permute-start | bytes 9224 | tf_op jit(solution)/shard_map/ppermute | solution.py:49
  182.8 4.9 %collective-permute-start.6 = (f32[19,1,16,128]{3,2,1,0:T(8,128)S(1)}, f32[19,1,16,128]{3,2,1,0:T(8,128)S(1)}, u32[]{:S(2)}, u32[]{:S(2)}) collective-permute-start(f32[19,1,16,128]{3,2,1,0:T(8,128)S(1)} %get-tuple-element.78), channel_id=1, source_target_pairs={{0,8},{8,16},{16,24},{1,9},{9,17},{17,25},{2,10},{10,18},{18,26},{... | collective-permute-start | bytes 466952 | tf_op jit(solution)/shard_map/ppermute | solution.py:48
  185.8 4.4 %collective-permute-start.7 = (f32[19,1,16,128]{3,2,1,0:T(8,128)S(1)}, f32[19,1,16,128]{3,2,1,0:T(8,128)S(1)}, u32[]{:S(2)}, u32[]{:S(2)}) collective-permute-start(f32[19,1,16,128]{3,2,1,0:T(8,128)S(1)} %get-tuple-element.77), channel_id=1, source_target_pairs={{8,0},{16,8},{24,16},{9,1},{17,9},{25,17},{10,2},{18,10},{26,18},{... | collective-permute-start | bytes 466952 | tf_op jit(solution)/shard_map/ppermute | solution.py:49
  190.3 4.4 %collective-permute-start.8 = (f32[19,10,1,128]{3,2,1,0:T(1,128)S(1)}, f32[19,10,1,128]{3,2,1,0:T(1,128)S(1)}, u32[]{:S(2)}, u32[]{:S(2)}) collective-permute-start(f32[19,10,1,128]{3,2,1,0:T(1,128)S(1)} %get-tuple-element.76), channel_id=1, source_target_pairs={{0,4},{1,5},{2,6},{3,7},{8,12},{9,13},{10,14},{11,15},{16,20},{17,... | collective-permute-start | bytes 291848 | tf_op jit(solution)/shard_map/ppermute | solution.py:48
  191.9 6.5 %collective-permute-start.9 = (f32[19,10,1,128]{3,2,1,0:T(1,128)S(1)}, f32[19,10,1,128]{3,2,1,0:T(1,128)S(1)}, u32[]{:S(2)}, u32[]{:S(2)}) collective-permute-start(f32[19,10,1,128]{3,2,1,0:T(1,128)S(1)} %get-tuple-element.75), channel_id=1, source_target_pairs={{4,0},{5,1},{6,2},{7,3},{12,8},{13,9},{14,10},{15,11},{20,16},{21,... | collective-permute-start | bytes 291848 | tf_op jit(solution)/shard_map/ppermute | solution.py:49
  204.5 10.4 %collective-permute-start.10 = (f32[19,10,18,1]{0,3,2,1:T(1,128)S(1)}, f32[19,10,18,1]{0,3,2,1:T(1,128)S(1)}, u32[]{:S(2)}, u32[]{:S(2)}) collective-permute-start(f32[19,10,18,1]{0,3,2,1:T(1,128)S(1)} %copy.177), channel_id=1, source_target_pairs={{0,1},{1,2},{2,3},{4,5},{5,6},{6,7},{8,9},{9,10},{10,11},{12,13},{... | collective-permute-start | bytes 41048 | tf_op jit(solution)/shard_map/ppermute | solution.py:48
  212.0 6.6 %collective-permute-start.11 = (f32[19,10,18,1]{0,3,2,1:T(1,128)S(1)}, f32[19,10,18,1]{0,3,2,1:T(1,128)S(1)}, u32[]{:S(2)}, u32[]{:S(2)}) collective-permute-start(f32[19,10,18,1]{0,3,2,1:T(1,128)S(1)} %copy.179), channel_id=1, source_target_pairs={{1,0},{2,1},{3,2},{5,4},{6,5},{7,6},{9,8},{10,9},{11,10},{13,12},{... | collective-permute-start | bytes 41048 | tf_op jit(solution)/shard_map/ppermute | solution.py:49
  (26 other events, 108.7 us)
where the time goes:
time: 237 us; the launch traced here: 233 us
  local copies, waits for them, and re-layouts  99.7 us (42%)
  starting transfers between devices  50.9 us (21%)
  other arithmetic  36 us (15%)
  waiting for transfers between devices  32.4 us (14%)
  matrix products  12.4 us (5%)
    gather x2, local copies, waits for them, and re-layouts, body(): solid_velocity = SPEED_UNIT * jnp.take(touch_velocity, intersection, axis=1)  65.4 us
    ppermute x12, starting transfers between devices, padded(): before = lax.ppermute(last, axis, up)  35.3 us
    ppermute x12, waiting for transfers between devices, padded(): after = lax.ppermute(first, axis, down)  30.5 us
    ppermute x12, starting transfers between devices, padded(): after = lax.ppermute(first, axis, down)  15.6 us
    unnamed x35, other arithmetic  14.6 us
    dot_general x1, matrix products, add_block(): jnp.einsum('dc,kc->dk', block_force, onehot, precision=lax.Precision.HIGH...  7.43 us
    slice x3, local copies, waits for them, and re-layouts, padded(): first = lax.slice_in_dim(shard, 0, width, axis=dim)  5.69 us
    unnamed x110, local copies, waits for them, and re-layouts  5.18 us
  transfers between devices with their start and end apart: 24, of which 10 were waited for; matrix products, arithmetic and copies ran while one was open for 17% of the time, Pallas kernels for 0%

commit v1 on v0

v1 whole, which is shorter than its diff:
```python
import jax
import jax.numpy as jnp
from jax import lax
from jax.experimental import pallas as pl
from jax.experimental.pallas import tpu as pltpu
from jax.sharding import PartitionSpec as P

R = 8


LATTICE = [
    (0, 0, 0),
    (1, 0, 0),
    (-1, 0, 0),
    (0, 1, 0),
    (0, -1, 0),
    (0, 0, 1),
    (0, 0, -1),
    (1, 1, 0),
    (-1, -1, 0),
    (1, -1, 0),
    (-1, 1, 0),
    (1, 0, 1),
    (-1, 0, -1),
    (1, 0, -1),
    (-1, 0, 1),
    (0, 1, 1),
    (0, -1, -1),
    (0, 1, -1),
    (0, -1, 1),
]
OPPOSITE = [0, 2, 1, 4, 3, 6, 5, 8, 7, 10, 9, 12, 11, 14, 13, 16, 15, 18, 17]
WEIGHTS = [1.0 / 3.0] + [1.0 / 18.0] * 6 + [1.0 / 36.0] * 12
RELAX_TIME = 0.8
SPEED_UNIT = 0.05
FORCE_SCALE = 0.1
CONTACT_GAIN = 1.0
GRAVITY_STEP = 0.1


F32 = jnp.float32
BF16 = jnp.bfloat16
SIDES = [[[i for i, c in enumerate(LATTICE) if c[dim] == sign] for sign in (-1, 1)] for dim in range(3)]
Z_DIRS = SIDES[2][1] + SIDES[2][0]
FACES = [(1, 0, 0), (-1, 0, 0), (0, 1, 0), (0, -1, 0), (0, 0, 1), (0, 0, -1)]
NT = (((1,), (1,)), ((), ()))


def outgoing(dim, sign):
    return SIDES[dim][1 if sign > 0 else 0]


def find(vector):
    return LATTICE.index(tuple(vector))


def split3(value):
    high = value.astype(BF16).astype(F32)
    rest = value - high
    middle = rest.astype(BF16).astype(F32)
    return high, middle, rest - middle


def solid_share(fraction, slots, touches):
    return jnp.where(
        slots < touches,
        fraction * (RELAX_TIME - 0.5) / (1.0 - fraction + (RELAX_TIME - 0.5)),
        0.0,
    )


def moments(f):
    density = f[0]
    for i in range(1, 19):
        density = density + f[i]
    momentum = []
    for dim in range(3):
        total = None
        for i in outgoing(dim, 1):
            pair = f[i] - f[OPPOSITE[i]]
            total = pair if total is None else total + pair
        momentum.append(total)
    return density, momentum


def sums_kernel(pop, fraction, slots, particles, touch, packet, vals, *, span_x, span_y, touches):
    width = pop.shape[2]
    for x in range(span_x):
        rows = pl.ds(x * span_y, span_y)
        f = [pop[i, rows, :] for i in range(19)]
        density, momentum = moments(f)
        share = solid_share(fraction[rows, :], slots[rows, :], touches)
        for q, field in enumerate(momentum + [density]):
            for s, part in enumerate(split3(share * field)):
                vals[pl.ds(x * span_y * 16 + s * 4 + q, span_y, stride=16), :] = part
        for j in range(12, 16):
            vals[pl.ds(x * span_y * 16 + j, span_y, stride=16), :] = jnp.zeros((span_y, width), F32)
    labels = lax.broadcasted_iota(jnp.int32, (touches, width), 0)
    group = 8

    def step(turn, total):
        block = slots[pl.ds(turn * group, group), :]
        left = []
        right = []
        for r in range(group):
            left.append(vals[pl.ds((turn * group + r) * 16, 16), :].astype(BF16))
            right.append(jnp.where(block[r : r + 1, :] == labels, 1.0, 0.0).astype(BF16))
        return total + lax.dot_general(
            jnp.concatenate(left, axis=1),
            jnp.concatenate(right, axis=1),
            NT,
            preferred_element_type=F32,
        )

    turns = span_x * span_y // group
    total = lax.fori_loop(0, turns, step, jnp.zeros((16, touches), F32), unroll=2)
    sums = total[0:4] + total[4:8] + total[8:12]
    halves = touches // width
    packet[0:6, :] = particles[...]
    packet[6 : 6 + halves, :] = touch[...].astype(F32)
    for h in range(halves):
        packet[6 + halves + 4 * h : 10 + halves + 4 * h, :] = sums[:, h * width : (h + 1) * width]


def lookup(table, index):
    return jnp.take_along_axis(table, index, axis=1)


def step_kernel(
    place, pop, fraction, slots, packets, touch, contacts, code, slot,
    relaxed, send, z_up, z_down, stay, speeds, columns,
    *, span_x, span_y, touches, mesh_shape,
):
    width = pop.shape[2]
    halves = touches // width
    neighbours = contacts.shape[0]
    n_x, n_y, n_z = mesh_shape
    lane = lax.broadcasted_iota(jnp.int32, (8, width), 1)
    sub = lax.broadcasted_iota(jnp.int32, (8, width), 0)
    base = packets.shape[1]
    me = (place[0] * n_y + place[1]) * n_z + place[2]
    own = packets[me, 0:8, :]
    tables = []
    labels = lax.broadcasted_iota(jnp.int32, (width, width), 0)
    force = [jnp.zeros((24, width), F32) for h in range(halves)]
    touched = [jnp.zeros((8, width), F32) for h in range(halves)]
    touch_entries = [touch[h : h + 1, :] for h in range(halves)]
    touch_code = [jnp.broadcast_to(t // width, (8, width)) for t in touch_entries]
    touch_slot = [jnp.broadcast_to(t % width, (8, width)) for t in touch_entries]
    contact_all = contacts[...]
    contact_code = contact_all // width
    contact_slot = contact_all % width
    picked = [jnp.zeros((8, width), F32) for n in range(neighbours)]
    shifts = (span_x / R, span_y / R, width / R)
    for c in range(27):
        o = (c // 9 - 1, c // 3 % 3 - 1, c % 3 - 1)
        p = [place[k] + o[k] for k in range(3)]
        valid = (
            (p[0] >= 0) & (p[0] < n_x) & (p[1] >= 0) & (p[1] < n_y) & (p[2] >= 0) & (p[2] < n_z)
        )
        index = jnp.where(valid, (p[0] * n_y + p[1]) * n_z + p[2], me)
        keep = valid.astype(F32)
        record = packets[index, 0:8, :] * keep
        for h in range(halves):
            got = lookup(record, touch_slot[h])
            touched[h] = jnp.where(touch_code[h] == c, got, touched[h])
        offset = jnp.where(sub == 0, o[0] * shifts[0], jnp.where(sub == 1, o[1] * shifts[1], jnp.where(sub == 2, o[2] * shifts[2], 0.0)))
        shifted = record + offset
        for n in range(neighbours):
            got = lookup(shifted, jnp.broadcast_to(contact_slot[n : n + 1, :], (8, width)))
            picked[n] = jnp.where(jnp.broadcast_to(contact_code[n : n + 1, :], (8, width)) == c, got, picked[n])
        entries = packets[index, 6 : 6 + halves, :].astype(jnp.int32)
        mine = jnp.where(entries // width == 26 - c, entries % width, -1)
        for h in range(halves):
            part = packets[index, 6 + halves + 4 * h : 10 + halves + 4 * h, :] * keep
            part = jnp.concatenate([part, jnp.zeros((4, width), F32)], axis=0)
            left = jnp.concatenate(list(split3(part)), axis=0).astype(BF16)
            right = jnp.where(mine[h : h + 1, :] == labels, 1.0, 0.0).astype(BF16)
            force[h] = force[h] + lax.dot_general(left, right, NT, preferred_element_type=F32)
    total = force[0]
    for h in range(1, halves):
        total = total + force[h]
    total = total[0:8] + total[8:16] + total[16:24]

    contact_force = jnp.zeros((8, width), F32)
    for n in range(neighbours):
        separation = jnp.where(sub < 3, own - picked[n], 0.0)
        square = jnp.sum(separation * separation, axis=0, keepdims=True)
        soften = 1.0 + 0.25 * square
        valid = jnp.where(contact_all[n : n + 1, :] < 27 * width, CONTACT_GAIN, 0.0)
        contact_force = contact_force + separation * (valid / (soften * soften))
    position = own[0:3]
    velocity = own[3:6]
    hydro = total[0:3] - SPEED_UNIT * velocity * total[3:4]
    gravity = jnp.where(sub[0:3] == 2, GRAVITY_STEP, 0.0)
    velocity_new = velocity + FORCE_SCALE * hydro + contact_force[0:3] - gravity
    position_new = position + velocity_new * (SPEED_UNIT / R)
    record = jnp.concatenate([position_new, velocity_new, jnp.zeros((2, width), F32)], axis=0)
    placing = jnp.where(slot[...] == labels, 1.0, 0.0).astype(BF16)
    arrive = []
    for o in [(0, 0, 0)] + FACES:
        offset = jnp.where(sub == 0, o[0] * shifts[0], jnp.where(sub == 1, o[1] * shifts[1], jnp.where(sub == 2, o[2] * shifts[2], 0.0)))
        chosen = jnp.where(code[...] == 13 + 9 * o[0] + 3 * o[1] + o[2], record - offset, 0.0)
        left = jnp.concatenate(list(split3(chosen)), axis=0).astype(BF16)
        out = lax.dot_general(left, placing, NT, preferred_element_type=F32)
        arrive.append(out[0:8] + out[8:16] + out[16:24])
    stay[...] = arrive[0]

    for h in range(halves):
        speeds[h, :, :] = SPEED_UNIT * touched[h]
    lane_y = lax.broadcasted_iota(jnp.int32, (span_y, width), 1)

    def slab(x, carry):
        rows = pl.ds(pl.multiple_of(x * span_y, span_y), span_y)
        f = [pop[i, rows, :] for i in range(19)]
        density, momentum = moments(f)
        index = slots[rows, :]
        share = solid_share(fraction[rows, :], index, touches)
        solid = []
        for dim in range(3):
            value = jnp.zeros((span_y, width), F32)
            for h in range(halves):
                line = jnp.broadcast_to(speeds[h, 3 + dim : 4 + dim, :], (span_y, width))
                got = lookup(line, index % width)
                value = jnp.where(index // width == h, got, value)
            solid.append(value)
        u = [m / density for m in momentum]
        rate = (1.0 - share) / RELAX_TIME
        fluid_base = 1.0 - 1.5 * (u[0] * u[0] + u[1] * u[1] + u[2] * u[2])
        solid_base = 1.0 - 1.5 * (solid[0] * solid[0] + solid[1] * solid[1] + solid[2] * solid[2])

        def project(i, v):
            value = None
            for dim in range(3):
                if LATTICE[i][dim]:
                    term = v[dim] if LATTICE[i][dim] > 0 else -v[dim]
                    value = term if value is None else value + term
            return value

        packed = jnp.zeros((span_y, width), F32)
        for i in range(19):
            j = OPPOSITE[i]
            if j < i:
                continue
            scale = WEIGHTS[i] * density
            if i == 0:
                fluid = scale * fluid_base
                results = [(0, f[0] - rate * (f[0] - fluid) + share * (scale * solid_base - fluid))]
            else:
                pu = project(i, u)
                ps = project(i, solid)
                even_u = fluid_base + 4.5 * pu * pu
                even_s = solid_base + 4.5 * ps * ps
                eq_i = scale * (even_u + 3.0 * pu)
                eq_j = scale * (even_u - 3.0 * pu)
                solid_i = scale * (even_s + 3.0 * ps)
                solid_j = scale * (even_s - 3.0 * ps)
                swap = f[j] - f[i]
                results = [
                    (i, f[i] - rate * (f[i] - eq_i) + share * (swap + solid_i - eq_j)),
                    (j, f[j] - rate * (f[j] - eq_j) + share * (solid_j - swap - eq_i)),
                ]
            for d, value in results:
                relaxed[d, rows, :] = value
                if LATTICE[d][2]:
                    k = Z_DIRS.index(d)
                    at = width - 1 if LATTICE[d][2] > 0 else 0
                    packed = jnp.where(lane_y == k, pltpu.roll(value, (k - at) % width, 1), packed)
        columns[rows, :] = packed
        return carry

    lax.fori_loop(0, span_x, slab, 0)
    z_rows = columns[...].T[0:16, :]
    z_up[0:8, :] = arrive[5]
    z_up[8:16, :] = jnp.concatenate([z_rows[0:5], jnp.zeros((3, width), F32)], axis=0)
    z_down[0:8, :] = arrive[6]
    z_down[8:16, :] = jnp.concatenate([z_rows[5:10], jnp.zeros((3, width), F32)], axis=0)
    send[...] = jnp.zeros(send.shape, F32)
    for o_x in (-1, 0, 1):
        for o_y in (-1, 0, 1):
            if o_x == 0 and o_y == 0:
                continue
            p_x = place[0] + o_x
            p_y = place[1] + o_y
            valid = (p_x >= 0) & (p_x < n_x) & (p_y >= 0) & (p_y < n_y)

            @pl.when(valid)
            def fill(o_x=o_x, o_y=o_y, index=p_x * n_y + p_y):
                x_at = span_x - 1 if o_x > 0 else 0
                y_at = span_y - 1 if o_y > 0 else 0
                if o_x and o_y:
                    row = x_at * span_y + y_at
                    send[index, 8:9, :] = relaxed[find((o_x, o_y, 0)), row : row + 1, :]
                    return
                n = FACES.index((o_x, o_y, 0))
                up = Z_DIRS.index(find((o_x, o_y, 1)))
                down = Z_DIRS.index(find((o_x, o_y, -1)))
                send[index, 0:8, :] = jnp.concatenate(
                    [arrive[1 + n][0:6], z_rows[up : up + 1], z_rows[down : down + 1]], axis=0
                )
                if o_x:
                    for k, d in enumerate(outgoing(0, o_x)):
                        send[index, 8 + k * span_y : 8 + (k + 1) * span_y, :] = relaxed[
                            d, x_at * span_y : (x_at + 1) * span_y, :
                        ]
                else:
                    for k, d in enumerate(outgoing(1, o_y)):
                        send[index, 8 + k * span_x : 8 + (k + 1) * span_x, :] = relaxed[
                            d, pl.ds(y_at, span_x, stride=span_y), :
                        ]


def pass_kernel(
    place, relaxed, got, z_below, z_above, stay, out, particles, filler,
    *, span_x, span_y, mesh_shape,
):
    width = relaxed.shape[2]
    n_x, n_y, n_z = mesh_shape
    cells = span_x * span_y

    def neighbour(o_x, o_y):
        p_x = jnp.clip(place[0] + o_x, 0, n_x - 1)
        p_y = jnp.clip(place[1] + o_y, 0, n_y - 1)
        return p_x * n_y + p_y

    def inside(axis, sign):
        p = place[axis] + sign
        return (p >= 0) & (p < mesh_shape[axis])

    arrived = stay[...] + z_below[0:8, :] + z_above[0:8, :]
    for o_x, o_y, o_z in FACES[:4]:
        axis = 0 if o_x else 1
        keep = inside(axis, o_x + o_y)
        arrived = arrived + jnp.where(keep, got[neighbour(o_x, o_y), 0:8, :], 0.0)
    particles[...] = arrived[0:6]

    lane1 = lax.broadcasted_iota(jnp.int32, (1, cells), 1)
    fills = []
    for d in Z_DIRS:
        c_x, c_y, c_z = LATTICE[d]
        source = z_below if c_z > 0 else z_above
        k = outgoing(2, c_z).index(d)
        row = source[8 + k : 9 + k, :]
        if c_x or c_y:
            edge = source[pl.ds(16 + neighbour(-c_x, -c_y), 1), :]
            if c_x:
                row = pltpu.roll(row, (c_x * span_y) % cells, 1)
                edge = pltpu.roll(edge, (c_x * span_y) % cells, 1)
                at_edge = lane1 < span_y if c_x > 0 else lane1 >= cells - span_y
            else:
                row = pltpu.roll(row, c_y % cells, 1)
                edge = pltpu.roll(edge, (-c_y * (span_y - 1)) % cells, 1)
                at_edge = lane1 % span_y == (0 if c_y > 0 else span_y - 1)
            row = jnp.where(at_edge, edge, row)
        fills.append(row)
    stacked = jnp.concatenate(fills + [jnp.zeros((cells - len(fills), cells), F32)], axis=0)
    filler[...] = stacked.T
    lane = lax.broadcasted_iota(jnp.int32, (span_y, width), 1)
    line = lax.broadcasted_iota(jnp.int32, (span_y, width), 0)
    for d, (c_x, c_y, c_z) in enumerate(LATTICE):
        y_in = inside(1, -c_y) if c_y else None
        z_in = inside(2, -c_z) if c_z else None
        for x in range(span_x):
            x_from = x - c_x
            crosses = x_from < 0 or x_from >= span_x
            if crosses:
                k = outgoing(0, c_x).index(d)
                value = got[neighbour(-c_x, 0), 8 + k * span_y : 8 + (k + 1) * span_y, :]
            else:
                value = relaxed[d, x_from * span_y : (x_from + 1) * span_y, :]
            outside = None
            if c_y:
                if crosses:
                    row = got[neighbour(-c_x, -c_y), 8:9, :]
                else:
                    at = 8 + outgoing(1, c_y).index(d) * span_x + x_from
                    row = got[neighbour(0, -c_y), at : at + 1, :]
                at_edge = line == (0 if c_y > 0 else span_y - 1)
                value = jnp.where(at_edge, row, pltpu.roll(value, c_y % span_y, 0))
                outside = at_edge & jnp.logical_not(y_in)
            if c_z:
                target = 0 if c_z > 0 else width - 1
                fill = pltpu.roll(
                    filler[x * span_y : (x + 1) * span_y, :], (target - Z_DIRS.index(d)) % width, 1
                )
                at_edge = lane == target
                value = jnp.where(at_edge, fill, pltpu.roll(value, c_z % width, 1))
                z_out = at_edge & jnp.logical_not(z_in)
                outside = z_out if outside is None else outside | z_out
            if crosses:
                x_out = jnp.broadcast_to(jnp.logical_not(inside(0, -c_x)), (span_y, width))
                outside = x_out if outside is None else outside | x_out
            if outside is not None:
                back = relaxed[OPPOSITE[d], x * span_y : (x + 1) * span_y, :]
                value = jnp.where(outside, back, value)
            out[d, x * span_y : (x + 1) * span_y, :] = value


def shape_of(*dims):
    return jax.ShapeDtypeStruct(dims, F32)


def call(kernel, outs, scratch, smem, *operands):
    vmem = pl.BlockSpec(memory_space=pltpu.VMEM)
    specs = [pl.BlockSpec(memory_space=pltpu.SMEM)] * smem + [vmem] * (len(operands) - smem)
    return pl.pallas_call(
        kernel,
        out_shape=outs,
        in_specs=specs,
        out_specs=jax.tree.map(lambda unused: vmem, outs),
        scratch_shapes=scratch,
    )(*operands)


def bind(kernel, **settings):
    def bound(*refs):
        return kernel(*refs, **settings)

    return bound


def body(
    populations, solid_fraction, intersection, touch, particles, contacts, dest_code, dest_slot
):
    unused, span_x, span_y, span_z = populations.shape
    particle_slots = particles.shape[4]
    touches = touch.shape[3]
    halves = touches // span_z
    neighbours = contacts.shape[3]
    cells = span_x * span_y
    axes = ("gx", "gy", "gz")
    mesh_shape = tuple(lax.axis_size(axis) for axis in axes)
    n_x, n_y, n_z = mesh_shape
    place = jnp.stack([lax.axis_index(axis) for axis in axes]).astype(jnp.int32)
    pop = populations.reshape(19, cells, span_z)
    fraction = solid_fraction.reshape(cells, span_z)
    slots = intersection.reshape(cells, span_z)
    records = particles.reshape(6, particle_slots)
    touch_rows = touch.reshape(halves, span_z)
    rows = 6 + 5 * halves
    packet = call(
        bind(sums_kernel, span_x=span_x, span_y=span_y, touches=touches),
        shape_of(rows, span_z),
        [pltpu.VMEM((cells * 16, span_z), F32)],
        0,
        pop, fraction, slots, records, touch_rows,
    )
    copies = jnp.broadcast_to(packet[None], (n_x * n_y * n_z, rows, span_z))
    packets = lax.all_to_all(copies, axes, 0, 0)
    chunk = 8 + 5 * max(span_x, span_y)
    relaxed, send, z_up, z_down, stay = call(
        bind(step_kernel, span_x=span_x, span_y=span_y, touches=touches, mesh_shape=mesh_shape),
        (
            shape_of(19, cells, span_z),
            shape_of(n_x * n_y, chunk, span_z),
            shape_of(16, span_z),
            shape_of(16, span_z),
            shape_of(8, span_z),
        ),
        [pltpu.VMEM((halves, 8, span_z), F32), pltpu.VMEM((cells, span_z), F32)],
        1,
        place, pop, fraction, slots, packets, touch_rows,
        contacts.reshape(neighbours, particle_slots),
        dest_code.reshape(1, particle_slots), dest_slot.reshape(1, particle_slots),
    )
    got = lax.all_to_all(send, ("gx", "gy"), 0, 0)
    up = [(i, i + 1) for i in range(n_z - 1)]
    down = [(j, i) for i, j in up]
    z_below = lax.ppermute(jnp.concatenate([z_up, got[:, 6]]), "gz", up)
    z_above = lax.ppermute(jnp.concatenate([z_down, got[:, 7]]), "gz", down)
    passed, arrived = call(
        bind(pass_kernel, span_x=span_x, span_y=span_y, mesh_shape=mesh_shape),
        (shape_of(19, cells, span_z), shape_of(6, span_z)),
        [pltpu.VMEM((cells, cells), F32)],
        1,
        place, relaxed, got, z_below, z_above, stay,
    )
    return passed.reshape(populations.shape), arrived.reshape(1, 1, 1, 6, particle_slots)


def solution(mesh):
    placed = (
        P(None, "gx", "gy", "gz"),
        P("gx", "gy", "gz"),
        P("gx", "gy", "gz"),
        P("gx", "gy", "gz", None),
        P("gx", "gy", "gz", None, None),
        P("gx", "gy", "gz", None, None),
        P("gx", "gy", "gz", None),
        P("gx", "gy", "gz", None),
    )
    return jax.shard_map(
        body,
        mesh=mesh,
        in_specs=placed,
        out_specs=(P(None, "gx", "gy", "gz"), P("gx", "gy", "gz", None, None)),
        check_vma=False,
    )
```

time: 237 us -> 59.1 us (0.25); the launches traced: 233 us -> 58.5 us
  local copies, waits for them, and re-layouts: 99.7 us -> 5.85 us
  starting transfers between devices: 50.9 us -> 10.7 us
  other arithmetic: 36 us -> 2.11 us
  waiting for transfers between devices: 32.4 us -> 13.7 us
  Pallas kernels: 0 us -> 14.4 us
  matrix products: 12.4 us -> 0 us
  blocking collectives: 0 us -> 11 us
    gather x4 -> x0, local copies, waits for them, and re-layouts: 70.9 us -> none  [the longest x2 65.4 us: body(): solid_velocity = SPEED_UNIT * jnp.take(touch_velocity, intersection, axis=1)]
    ppermute x24 -> x2, starting transfers between devices: 50.9 us -> 3.34 us  [the longest x1 2.06 us: body(): z_below = lax.ppermute(jnp.concatenate([z_up, got[:, 6]]), 'gz', up)]
    ppermute x24 -> x2, waiting for transfers between devices: 32.4 us -> 4.27 us  [the longest x1 4.27 us: body(): z_above = lax.ppermute(jnp.concatenate([z_down, got[:, 7]]), 'gz', down)]
    unnamed x35 -> x0, other arithmetic: 14.6 us -> none
    pallas_call x0 -> x3, Pallas kernels: none -> 14.4 us  [call(): pl.pallas_call(kernel, out_shape=outs, in_specs=specs, out_specs=jax.tree...]
    slice x19 -> x1, local copies, waits for them, and re-layouts: 13.2 us -> 0.01 us  [body(): z_above = lax.ppermute(jnp.concatenate([z_down, got[:, 7]]), 'gz', down)]
    dot_general x5 -> x0, matrix products: 12.4 us -> none  [the longest x1 7.43 us: add_block(): jnp.einsum('dc,kc->dk', block_force, onehot, precision=lax.Precision.HIGH...]
    all_to_all x0 -> x1, blocking collectives: none -> 11 us  [body(): got = lax.all_to_all(send, ('gx', 'gy'), 0, 0)]
  transfers between devices with their start and end apart: 24 -> 3, of which waited for: 10 -> 2; matrix products, arithmetic and copies ran while one was open for 17% -> 3% of each run, Pallas kernels for 0% -> 0%
where the time goes in v1:
time: 59.1 us; the launch traced here: 58.5 us
  Pallas kernels  14.4 us (24%)
  waiting for transfers between devices  13.7 us (23%)
  blocking collectives  11 us (19%)
  starting transfers between devices  10.7 us (18%)
  local copies, waits for them, and re-layouts  5.85 us (10%)
  other arithmetic  2.11 us (4%)
  between operations  0.71 us (1%)
    pallas_call x3, Pallas kernels, call(): pl.pallas_call(kernel, out_shape=outs, in_specs=specs, out_specs=jax.tree...  14.4 us
    all_to_all x1, blocking collectives, body(): got = lax.all_to_all(send, ('gx', 'gy'), 0, 0)  11 us
    all_to_all x1, waiting for transfers between devices, body(): packets = lax.all_to_all(copies, axes, 0, 0)  9.47 us
    all_to_all x1, starting transfers between devices, body(): packets = lax.all_to_all(copies, axes, 0, 0)  7.33 us
    unnamed x13, local copies, waits for them, and re-layouts  4.42 us
    ppermute x1, waiting for transfers between devices, body(): z_above = lax.ppermute(jnp.concatenate([z_down, got[:, 7]]), 'gz', down)  4.27 us
    ppermute x1, starting transfers between devices, body(): z_below = lax.ppermute(jnp.concatenate([z_up, got[:, 6]]), 'gz', up)  2.06 us
    broadcast_in_dim x1, local copies, waits for them, and re-layouts, body(): copies = jnp.broadcast_to(packet[None], (n_x * n_y * n_z, rows, span_z))  1.42 us
  transfers between devices with their start and end apart: 3, of which 2 were waited for; matrix products, arithmetic and copies ran while one was open for 3% of the time, Pallas kernels for 0%

profile of v1, /device:TPU:0, one launch (start us, length us, event | category | flops | bytes accessed | tf_op | source)
XLA Modules:
  0.0 58.5 jit_solution(9621090302355684034)
XLA Ops:
  0.6 0.0 copy-start.4
  0.6 1.3 %copy.23 = f32[1,1,1,6,128]{4,3,2,1,0:T(8,128)} copy(f32[1,1,1,6,128]{4,2,3,1,0:T(1,128)} %param.12) | data formatting | bytes 6144
  1.9 5.5 %shard_map.95 = f32[16,128]{1,0:T(8,128)} custom-call(f32[19,128,128]{2,1,0:T(8,128)} %bitcast.23, f32[128,128]{1,0:T(8,128)} %bitcast.25, s32[128,128]{1,0:T(8,128)} %bitcast.27, f32[6,128]{1,0:T(8,128)} %bitcast.30, s32[2,128]{1,0:T(2,128)} %bitcast.33), custom_call_target="tpu_custom_call" | custom-call | tf_op jit(solution)/shard_map/pallas_call | solution.py:406
  7.4 1.4 %broadcast_in_dim.2 = f32[32,16,128]{2,1,0:T(8,128)} broadcast(f32[16,128]{1,0:T(8,128)} %shard_map.95), dimensions={1,2} | broadcast | bytes 270336 | tf_op jit(solution)/shard_map/broadcast_in_dim | solution.py:448
  8.8 7.3 %all-to-all-start = ((f32[32,16,128]{2,1,0:T(8,128)}), f32[32,16,128]{2,1,0:T(8,128)S(1)}, u32[]{:S(2)}, u32[]{:S(2)}) async-start(f32[32,16,128]{2,1,0:T(8,128)} %broadcast_in_dim.2), calls=%async_computation | async-start | bytes 524288 | tf_op jit(solution)/shard_map/all_to_all | solution.py:449
  16.1 0.0 copy-done.4
  16.2 0.6 %copy.22 = s32[1,1,1,12,128]{4,3,2,1,0:T(8,128)} copy(s32[1,1,1,12,128]{4,2,3,1,0:T(1,128)S(1)} %copy-done.4) | data formatting | bytes 12288
  16.8 0.7 %pad_add_fusion.refs_0_ = s32[3]{0:T(128)} fusion(s32[1]{0:T(128)} %bitcast.2, s32[1]{0:T(128)} %bitcast.1, s32[1]{0:T(128)} %bitcast), kind=kLoop, calls=%fused_computation.4 | loop fusion | flops 6 | bytes 24 | tf_op jit(solution)/shard_map/stack | solution.py:434
  17.4 9.5 %all-to-all-done.refs_4_ = f32[32,16,128]{2,1,0:T(8,128)S(1)} async-done(((f32[32,16,128]{2,1,0:T(8,128)}), f32[32,16,128]{2,1,0:T(8,128)S(1)}, u32[]{:S(2)}, u32[]{:S(2)}) %all-to-all-start) | async-done | bytes 262176 | tf_op jit(solution)/shard_map/all_to_all | solution.py:449
  26.9 0.0 copy-start.1
  26.9 0.7 %copy-done.1 = f32[32,16,128]{2,1,0:T(8,128)} copy-done((f32[32,16,128]{2,1,0:T(8,128)}, f32[32,16,128]{2,1,0:T(8,128)S(1)}, u32[]{:S(2)}) %copy-start.1) | copy-done | bytes 262168
  27.6 6.0 %shard_map.96 = (f32[19,128,128]{2,1,0:T(8,128)}, f32[8,88,128]{2,1,0:T(8,128)}, f32[16,128]{1,0:T(8,128)}, f32[16,128]{1,0:T(8,128)}, f32[8,128]{1,0:T(8,128)}) custom-call(s32[3]{0:T(128)} %pad_add_fusion.refs_0_, f32[19,128,128]{2,1,0:T(8,128)} %bitcast.24, f32[128,128]{1,0:T(8,128)} %bitcast.26, s32[128,128]{1,0:T(8,128)} %bitcast.28, ...), custom_call_target="tpu_custom_call" | custom-call | tf_op jit(solution)/shard_map/pallas_call | solution.py:406
  33.5 11.0 %all_to_all.10.refs_2_ = f32[8,88,128]{2,1,0:T(8,128)S(1)} all-to-all(f32[8,88,128]{2,1,0:T(8,128)} %get-tuple-element.10), channel_id=1, replica_groups=mesh['gx'=4,'gy'=2,'gz'=4] {'gx','gy'}, dimensions={0} | all-to-all | bytes 720896 | tf_op jit(solution)/shard_map/all_to_all | solution.py:466
  44.6 0.0 copy-start
  44.6 0.7 %pad_maximum_fusion = f32[24,128]{1,0:T(8,128)S(1)} fusion(f32[8,128]{1,0:T(8,128)S(1)} %bitcast.32, f32[16,128]{1,0:T(8,128)} %get-tuple-element.11), kind=kLoop, calls=%fused_computation | loop fusion | flops 3072 | bytes 24576 | tf_op jit(solution)/shard_map/concatenate | solution.py:469
  45.3 2.1 %collective-permute-start = (f32[24,128]{1,0:T(8,128)S(1)}, f32[24,128]{1,0:T(8,128)S(1)}, u32[]{:S(2)}, u32[]{:S(2)}) collective-permute-start(f32[24,128]{1,0:T(8,128)S(1)} %pad_maximum_fusion), channel_id=1, source_target_pairs={{0,1},{1,2},{2,3},{4,5},{5,6},{6,7},{8,9},{9,10},{10,11},{12,13},{... | collective-permute-start | bytes 36872 | tf_op jit(solution)/shard_map/ppermute | solution.py:469
  47.4 0.7 %pad_maximum_fusion.1 = f32[24,128]{1,0:T(8,128)S(1)} fusion(f32[8,128]{1,0:T(8,128)S(1)} %bitcast.31, f32[16,128]{1,0:T(8,128)} %get-tuple-element.12), kind=kLoop, calls=%fused_computation.1 | loop fusion | flops 3072 | bytes 24576 | tf_op jit(solution)/shard_map/concatenate | solution.py:470
  48.1 1.3 %collective-permute-start.1 = (f32[24,128]{1,0:T(8,128)S(1)}, f32[24,128]{1,0:T(8,128)S(1)}, u32[]{:S(2)}, u32[]{:S(2)}) collective-permute-start(f32[24,128]{1,0:T(8,128)S(1)} %pad_maximum_fusion.1), channel_id=1, source_target_pairs={{1,0},{2,1},{3,2},{5,4},{6,5},{7,6},{9,8},{10,9},{11,10},{13,12},{... | collective-permute-start | bytes 36872 | tf_op jit(solution)/shard_map/ppermute | solution.py:470
  49.4 0.0 collective-permute-done.refs_3_
  49.4 0.0 copy-start.2
  49.4 4.3 %collective-permute-done.1.refs_4_ = f32[24,128]{1,0:T(8,128)S(1)} collective-permute-done((f32[24,128]{1,0:T(8,128)S(1)}, f32[24,128]{1,0:T(8,128)S(1)}, u32[]{:S(2)}, u32[]{:S(2)}) %collective-permute-start.1) | collective-permute-done | bytes 12320 | tf_op jit(solution)/shard_map/ppermute | solution.py:470
  53.7 0.0 copy-start.3
  53.7 0.0 copy-done
  53.7 0.0 copy-done.2
  53.7 0.6 %copy-done.3 = f32[24,128]{1,0:T(8,128)} copy-done((f32[24,128]{1,0:T(8,128)}, f32[24,128]{1,0:T(8,128)S(1)}, u32[]{:S(2)}) %copy-start.3) | copy-done | bytes 12312
  54.3 3.0 %shard_map.97 = (f32[19,128,128]{2,1,0:T(8,128)}, f32[6,128]{1,0:T(8,128)}) custom-call(s32[3]{0:T(128)} %pad_add_fusion.refs_0_, f32[19,128,128]{2,1,0:T(8,128)} %get-tuple-element.9.refs_1_, f32[8,88,128]{2,1,0:T(8,128)} %copy-done, f32[24,128]{1,0:T(8,128)} %copy-done.2, f32[24,128]{1,0:T(8,128)} %copy-done.3, f32[8,128]{1,0:T(8,128)} %get-tuple-element.13.refs_5_), custom_call_target="tpu_custom_call" | custom-call | tf_op jit(solution)/shard_map/pallas_call | solution.py:406
  57.3 1.3 %copy.15 = f32[1,1,1,6,128]{4,2,3,1,0:T(1,128)} copy(f32[1,1,1,6,128]{4,3,2,1,0:T(8,128)} %bitcast.35) | data formatting | bytes 6144
  (1 shorter events, 0.0 us)
Async XLA Ops:
  0.6 15.5 %copy-start.4 = (s32[1,1,1,12,128]{4,2,3,1,0:T(1,128)S(1)}, s32[1,1,1,12,128]{4,2,3,1,0:T(1,128)}, u32[]{:S(2)}) copy-start(s32[1,1,1,12,128]{4,2,3,1,0:T(1,128)} %param.13) | copy-start | bytes 18436
  8.8 18.1 %all-to-all-start = ((f32[32,16,128]{2,1,0:T(8,128)}), f32[32,16,128]{2,1,0:T(8,128)S(1)}, u32[]{:S(2)}, u32[]{:S(2)}) async-start(f32[32,16,128]{2,1,0:T(8,128)} %broadcast_in_dim.2), calls=%async_computation | async-start | bytes 524288 | tf_op jit(solution)/shard_map/all_to_all | solution.py:449
  26.9 0.7 %copy-start.1 = (f32[32,16,128]{2,1,0:T(8,128)}, f32[32,16,128]{2,1,0:T(8,128)S(1)}, u32[]{:S(2)}) copy-start(f32[32,16,128]{2,1,0:T(8,128)S(1)} %all-to-all-done.refs_4_) | copy-start | bytes 786436
  44.6 9.1 %copy-start = (f32[8,88,128]{2,1,0:T(8,128)}, f32[8,88,128]{2,1,0:T(8,128)S(1)}, u32[]{:S(2)}) copy-start(f32[8,88,128]{2,1,0:T(8,128)S(1)} %all_to_all.10.refs_2_) | copy-start | bytes 1081348
  45.3 4.1 %collective-permute-start = (f32[24,128]{1,0:T(8,128)S(1)}, f32[24,128]{1,0:T(8,128)S(1)}, u32[]{:S(2)}, u32[]{:S(2)}) collective-permute-start(f32[24,128]{1,0:T(8,128)S(1)} %pad_maximum_fusion), channel_id=1, source_target_pairs={{0,1},{1,2},{2,3},{4,5},{5,6},{6,7},{8,9},{9,10},{10,11},{12,13},{... | collective-permute-start | bytes 36872 | tf_op jit(solution)/shard_map/ppermute | solution.py:469
  48.1 5.6 %collective-permute-start.1 = (f32[24,128]{1,0:T(8,128)S(1)}, f32[24,128]{1,0:T(8,128)S(1)}, u32[]{:S(2)}, u32[]{:S(2)}) collective-permute-start(f32[24,128]{1,0:T(8,128)S(1)} %pad_maximum_fusion.1), channel_id=1, source_target_pairs={{1,0},{2,1},{3,2},{5,4},{6,5},{7,6},{9,8},{10,9},{11,10},{13,12},{... | collective-permute-start | bytes 36872 | tf_op jit(solution)/shard_map/ppermute | solution.py:470
  49.4 4.3 %copy-start.2 = (f32[24,128]{1,0:T(8,128)}, f32[24,128]{1,0:T(8,128)S(1)}, u32[]{:S(2)}) copy-start(f32[24,128]{1,0:T(8,128)S(1)} %collective-permute-done.refs_3_) | copy-start | bytes 36868
  53.7 0.6 %copy-start.3 = (f32[24,128]{1,0:T(8,128)}, f32[24,128]{1,0:T(8,128)S(1)}, u32[]{:S(2)}) copy-start(f32[24,128]{1,0:T(8,128)S(1)} %collective-permute-done.1.refs_4_) | copy-start | bytes 36868

commit v2 on v1

--- a/solution.py
+++ b/solution.py
@@ -83,10 +83,21 @@
     return density, momentum
 
 
-def sums_kernel(pop, fraction, slots, particles, touch, packet, vals, *, span_x, span_y, touches):
+def sums_kernel(
+    source, fraction, slots, particles, touch, packets, vals, pop, arrivals,
+    *, span_x, span_y, touches,
+):
     width = pop.shape[2]
+    fetches = []
+    for x in range(span_x):
+        part = pl.ds(x * span_y, span_y)
+        fetches.append(
+            pltpu.make_async_copy(source.at[:, part], pop.at[:, part], arrivals.at[x])
+        )
+        fetches[x].start()
     for x in range(span_x):
         rows = pl.ds(x * span_y, span_y)
+        fetches[x].wait()
         f = [pop[i, rows, :] for i in range(19)]
         density, momentum = moments(f)
         share = solid_share(fraction[rows, :], slots[rows, :], touches)
@@ -116,10 +127,12 @@
     total = lax.fori_loop(0, turns, step, jnp.zeros((16, touches), F32), unroll=2)
     sums = total[0:4] + total[4:8] + total[8:12]
     halves = touches // width
-    packet[0:6, :] = particles[...]
-    packet[6 : 6 + halves, :] = touch[...].astype(F32)
+    parts = [particles[...], touch[...].astype(F32)]
     for h in range(halves):
-        packet[6 + halves + 4 * h : 10 + halves + 4 * h, :] = sums[:, h * width : (h + 1) * width]
+        parts.append(sums[:, h * width : (h + 1) * width])
+    packet = jnp.concatenate(parts, axis=0)
+    for n in range(packets.shape[0]):
+        packets[n, :, :] = packet
 
 
 def lookup(table, index):
@@ -310,54 +323,27 @@
                         ]
 
 
-def pass_kernel(
-    place, relaxed, got, z_below, z_above, stay, out, particles, filler,
-    *, span_x, span_y, mesh_shape,
-):
-    width = relaxed.shape[2]
-    n_x, n_y, n_z = mesh_shape
-    cells = span_x * span_y
-
+def locators(place, mesh_shape):
     def neighbour(o_x, o_y):
-        p_x = jnp.clip(place[0] + o_x, 0, n_x - 1)
-        p_y = jnp.clip(place[1] + o_y, 0, n_y - 1)
-        return p_x * n_y + p_y
+        p_x = jnp.clip(place[0] + o_x, 0, mesh_shape[0] - 1)
+        p_y = jnp.clip(place[1] + o_y, 0, mesh_shape[1] - 1)
+        return p_x * mesh_shape[1] + p_y
 
     def inside(axis, sign):
         p = place[axis] + sign
         return (p >= 0) & (p < mesh_shape[axis])
 
-    arrived = stay[...] + z_below[0:8, :] + z_above[0:8, :]
-    for o_x, o_y, o_z in FACES[:4]:
-        axis = 0 if o_x else 1
-        keep = inside(axis, o_x + o_y)
-        arrived = arrived + jnp.where(keep, got[neighbour(o_x, o_y), 0:8, :], 0.0)
-    particles[...] = arrived[0:6]
-
-    lane1 = lax.broadcasted_iota(jnp.int32, (1, cells), 1)
-    fills = []
-    for d in Z_DIRS:
-        c_x, c_y, c_z = LATTICE[d]
-        source = z_below if c_z > 0 else z_above
-        k = outgoing(2, c_z).index(d)
-        row = source[8 + k : 9 + k, :]
-        if c_x or c_y:
-            edge = source[pl.ds(16 + neighbour(-c_x, -c_y), 1), :]
-            if c_x:
-                row = pltpu.roll(row, (c_x * span_y) % cells, 1)
-                edge = pltpu.roll(edge, (c_x * span_y) % cells, 1)
-                at_edge = lane1 < span_y if c_x > 0 else lane1 >= cells - span_y
-            else:
-                row = pltpu.roll(row, c_y % cells, 1)
-                edge = pltpu.roll(edge, (-c_y * (span_y - 1)) % cells, 1)
-                at_edge = lane1 % span_y == (0 if c_y > 0 else span_y - 1)
-            row = jnp.where(at_edge, edge, row)
-        fills.append(row)
-    stacked = jnp.concatenate(fills + [jnp.zeros((cells - len(fills), cells), F32)], axis=0)
-    filler[...] = stacked.T
+    return neighbour, inside
+
+
+def pass_on(place, relaxed, got, filler, out, staged, sent, dirs, span_x, span_y, mesh_shape):
+    width = relaxed.shape[2]
+    neighbour, inside = locators(place, mesh_shape)
     lane = lax.broadcasted_iota(jnp.int32, (span_y, width), 1)
     line = lax.broadcasted_iota(jnp.int32, (span_y, width), 0)
-    for d, (c_x, c_y, c_z) in enumerate(LATTICE):
+    copies = []
+    for n, d in enumerate(dirs):
+        c_x, c_y, c_z = LATTICE[d]
         y_in = inside(1, -c_y) if c_y else None
         z_in = inside(2, -c_z) if c_z else None
         for x in range(span_x):
@@ -393,22 +379,74 @@
             if outside is not None:
                 back = relaxed[OPPOSITE[d], x * span_y : (x + 1) * span_y, :]
                 value = jnp.where(outside, back, value)
-            out[d, x * span_y : (x + 1) * span_y, :] = value
+            staged[n, x * span_y : (x + 1) * span_y, :] = value
+        copies.append(pltpu.make_async_copy(staged.at[n], out.at[d], sent.at[n]))
+        copies[n].start()
+    for copy in copies:
+        copy.wait()
+
+
+def flat_kernel(place, relaxed, got, out, staged, sent, *, span_x, span_y, mesh_shape):
+    dirs = [d for d in range(19) if LATTICE[d][2] == 0]
+    pass_on(place, relaxed, got, None, out, staged, sent, dirs, span_x, span_y, mesh_shape)
+
+
+def pass_kernel(
+    place, relaxed, got, z_below, z_above, stay, unused, out, particles, filler, staged, sent,
+    *, span_x, span_y, mesh_shape,
+):
+    cells = span_x * span_y
+    neighbour, inside = locators(place, mesh_shape)
+    arrived = stay[...] + z_below[0:8, :] + z_above[0:8, :]
+    for o_x, o_y, o_z in FACES[:4]:
+        axis = 0 if o_x else 1
+        keep = inside(axis, o_x + o_y)
+        arrived = arrived + jnp.where(keep, got[neighbour(o_x, o_y), 0:8, :], 0.0)
+    particles[...] = arrived[0:6]
+
+    lane1 = lax.broadcasted_iota(jnp.int32, (1, cells), 1)
+    fills = []
+    for d in Z_DIRS:
+        c_x, c_y, c_z = LATTICE[d]
+        source = z_below if c_z > 0 else z_above
+        k = outgoing(2, c_z).index(d)
+        row = source[8 + k : 9 + k, :]
+        if c_x or c_y:
+            edge = source[pl.ds(16 + neighbour(-c_x, -c_y), 1), :]
+            if c_x:
+                row = pltpu.roll(row, (c_x * span_y) % cells, 1)
+                edge = pltpu.roll(edge, (c_x * span_y) % cells, 1)
+                at_edge = lane1 < span_y if c_x > 0 else lane1 >= cells - span_y
+            else:
+                row = pltpu.roll(row, c_y % cells, 1)
+                edge = pltpu.roll(edge, (-c_y * (span_y - 1)) % cells, 1)
+                at_edge = lane1 % span_y == (0 if c_y > 0 else span_y - 1)
+            row = jnp.where(at_edge, edge, row)
+        fills.append(row)
+    stacked = jnp.concatenate(fills + [jnp.zeros((cells - len(fills), cells), F32)], axis=0)
+    filler[...] = stacked.T
+    pass_on(
+        place, relaxed, got, filler, out, staged, sent, Z_DIRS, span_x, span_y, mesh_shape
+    )
 
 
 def shape_of(*dims):
     return jax.ShapeDtypeStruct(dims, F32)
 
 
-def call(kernel, outs, scratch, smem, *operands):
-    vmem = pl.BlockSpec(memory_space=pltpu.VMEM)
-    specs = [pl.BlockSpec(memory_space=pltpu.SMEM)] * smem + [vmem] * (len(operands) - smem)
+VMEM = pl.BlockSpec(memory_space=pltpu.VMEM)
+SMEM = pl.BlockSpec(memory_space=pltpu.SMEM)
+HBM = pl.BlockSpec(memory_space=pltpu.HBM)
+
+
+def call(kernel, outs, out_specs, scratch, specs, *operands, aliases={}):
     return pl.pallas_call(
         kernel,
         out_shape=outs,
         in_specs=specs,
-        out_specs=jax.tree.map(lambda unused: vmem, outs),
+        out_specs=out_specs,
         scratch_shapes=scratch,
+        input_output_aliases=aliases,
     )(*operands)
 
 
@@ -438,14 +476,18 @@
     records = particles.reshape(6, particle_slots)
     touch_rows = touch.reshape(halves, span_z)
     rows = 6 + 5 * halves
-    packet = call(
+    copies = call(
         bind(sums_kernel, span_x=span_x, span_y=span_y, touches=touches),
-        shape_of(rows, span_z),
-        [pltpu.VMEM((cells * 16, span_z), F32)],
-        0,
+        shape_of(n_x * n_y * n_z, rows, span_z),
+        VMEM,
+        [
+            pltpu.VMEM((cells * 16, span_z), F32),
+            pltpu.VMEM((19, cells, span_z), F32),
+            pltpu.SemaphoreType.DMA((span_x,)),
+        ],
+        [HBM] + [VMEM] * 4,
         pop, fraction, slots, records, touch_rows,
     )
-    copies = jnp.broadcast_to(packet[None], (n_x * n_y * n_z, rows, span_z))
     packets = lax.all_to_all(copies, axes, 0, 0)
     chunk = 8 + 5 * max(span_x, span_y)
     relaxed, send, z_up, z_down, stay = call(
@@ -457,8 +499,9 @@
             shape_of(16, span_z),
             shape_of(8, span_z),
         ),
+        (VMEM,) * 5,
         [pltpu.VMEM((halves, 8, span_z), F32), pltpu.VMEM((cells, span_z), F32)],
-        1,
+        [SMEM] + [VMEM] * 8,
         place, pop, fraction, slots, packets, touch_rows,
         contacts.reshape(neighbours, particle_slots),
         dest_code.reshape(1, particle_slots), dest_slot.reshape(1, particle_slots),
@@ -468,12 +511,26 @@
     down = [(j, i) for i, j in up]
     z_below = lax.ppermute(jnp.concatenate([z_up, got[:, 6]]), "gz", up)
     z_above = lax.ppermute(jnp.concatenate([z_down, got[:, 7]]), "gz", down)
+    flat = call(
+        bind(flat_kernel, span_x=span_x, span_y=span_y, mesh_shape=mesh_shape),
+        shape_of(19, cells, span_z),
+        HBM,
+        [pltpu.VMEM((9, cells, span_z), F32), pltpu.SemaphoreType.DMA((9,))],
+        [SMEM, VMEM, VMEM],
+        place, relaxed, got,
+    )
     passed, arrived = call(
         bind(pass_kernel, span_x=span_x, span_y=span_y, mesh_shape=mesh_shape),
         (shape_of(19, cells, span_z), shape_of(6, span_z)),
-        [pltpu.VMEM((cells, cells), F32)],
-        1,
-        place, relaxed, got, z_below, z_above, stay,
+        (HBM, VMEM),
+        [
+            pltpu.VMEM((cells, cells), F32),
+            pltpu.VMEM((10, cells, span_z), F32),
+            pltpu.SemaphoreType.DMA((10,)),
+        ],
+        [SMEM] + [VMEM] * 5 + [HBM],
+        place, relaxed, got, z_below, z_above, stay, flat,
+        aliases={6: 0},
     )
     return passed.reshape(populations.shape), arrived.reshape(1, 1, 1, 6, particle_slots)
 

time: 59.1 us -> 58.8 us (level)
  Pallas kernels: 14.4 us -> 17.7 us
  waiting for transfers between devices: 13.7 us -> 11.5 us
  local copies, waits for them, and re-layouts: 5.85 us -> 4.43 us
    pallas_call x3 -> x4, Pallas kernels: 14.4 us -> 17.7 us  [call(): pl.pallas_call(kernel, out_shape=outs, in_specs=specs, out_specs=out_spec...]
    ppermute x1, waiting for transfers between devices: 4.27 us -> 2 us  [body(): z_above = lax.ppermute(jnp.concatenate([z_down, got[:, 7]]), 'gz', down)]
    broadcast_in_dim x1 -> x0, local copies, waits for them, and re-layouts: 1.42 us -> none  [body(): copies = jnp.broadcast_to(packet[None], (n_x * n_y * n_z, rows, span_z))]
  transfers between devices with their start and end apart: 3 -> 3, of which waited for: 2 -> 2; matrix products, arithmetic and copies ran while one was open for 3% -> 3% of each run, Pallas kernels for 0% -> 4%
where the time goes in v2:
time: 58.8 us; the launch traced here: 58.1 us
  Pallas kernels  17.7 us (30%)
  waiting for transfers between devices  11.5 us (20%)
  blocking collectives  11 us (19%)
  starting transfers between devices  10.7 us (18%)
  local copies, waits for them, and re-layouts  4.43 us (8%)
  other arithmetic  2.11 us (4%)
  between operations  0.73 us (1%)
    pallas_call x4, Pallas kernels, call(): pl.pallas_call(kernel, out_shape=outs, in_specs=specs, out_specs=out_spec...  17.7 us
    all_to_all x1, blocking collectives, body(): got = lax.all_to_all(send, ('gx', 'gy'), 0, 0)  11 us
    all_to_all x1, waiting for transfers between devices, body(): packets = lax.all_to_all(copies, axes, 0, 0)  9.47 us
    all_to_all x1, starting transfers between devices, body(): packets = lax.all_to_all(copies, axes, 0, 0)  7.33 us
    unnamed x13, local copies, waits for them, and re-layouts  4.42 us
    ppermute x1, starting transfers between devices, body(): z_below = lax.ppermute(jnp.concatenate([z_up, got[:, 6]]), 'gz', up)  2.06 us
    ppermute x1, waiting for transfers between devices, body(): z_above = lax.ppermute(jnp.concatenate([z_down, got[:, 7]]), 'gz', down)  2 us
    ppermute x1, starting transfers between devices, body(): z_above = lax.ppermute(jnp.concatenate([z_down, got[:, 7]]), 'gz', down)  1.28 us
  transfers between devices with their start and end apart: 3, of which 2 were waited for; matrix products, arithmetic and copies ran while one was open for 3% of the time, Pallas kernels for 4%

profile of v2, /device:TPU:0, one launch (start us, length us, event | category | flops | bytes accessed | tf_op | source)
XLA Modules:
  0.0 58.1 jit_solution(13426245700695553355)
XLA Ops:
  0.6 0.0 copy-start.4
  0.6 1.3 %copy.25 = f32[1,1,1,6,128]{4,3,2,1,0:T(8,128)} copy(f32[1,1,1,6,128]{4,2,3,1,0:T(1,128)} %param.12) | data formatting | bytes 6144
  1.9 6.2 %shard_map.95 = f32[32,16,128]{2,1,0:T(8,128)} custom-call(f32[19,128,128]{2,1,0:T(8,128)} %bitcast.23, f32[128,128]{1,0:T(8,128)} %bitcast.26, s32[128,128]{1,0:T(8,128)} %bitcast.28, f32[6,128]{1,0:T(8,128)} %bitcast.31, s32[2,128]{1,0:T(2,128)} %bitcast.35), custom_call_target="tpu_custom_call" | custom-call | tf_op jit(solution)/shard_map/pallas_call | solution.py:443
  8.2 7.3 %all-to-all-start = ((f32[32,16,128]{2,1,0:T(8,128)}), f32[32,16,128]{2,1,0:T(8,128)S(1)}, u32[]{:S(2)}, u32[]{:S(2)}) async-start(f32[32,16,128]{2,1,0:T(8,128)} %shard_map.95), calls=%async_computation | async-start | bytes 524288 | tf_op jit(solution)/shard_map/all_to_all | solution.py:491
  15.5 0.0 copy-done.4
  15.5 0.6 %copy.24 = s32[1,1,1,12,128]{4,3,2,1,0:T(8,128)} copy(s32[1,1,1,12,128]{4,2,3,1,0:T(1,128)S(1)} %copy-done.4) | data formatting | bytes 12288
  16.1 0.7 %pad_add_fusion.refs_0_ = s32[3]{0:T(128)} fusion(s32[1]{0:T(128)} %bitcast.2, s32[1]{0:T(128)} %bitcast.1, s32[1]{0:T(128)} %bitcast), kind=kLoop, calls=%fused_computation.4 | loop fusion | flops 6 | bytes 24 | tf_op jit(solution)/shard_map/stack | solution.py:472
  16.8 9.5 %all-to-all-done.refs_4_ = f32[32,16,128]{2,1,0:T(8,128)S(1)} async-done(((f32[32,16,128]{2,1,0:T(8,128)}), f32[32,16,128]{2,1,0:T(8,128)S(1)}, u32[]{:S(2)}, u32[]{:S(2)}) %all-to-all-start) | async-done | bytes 262176 | tf_op jit(solution)/shard_map/all_to_all | solution.py:491
  26.2 0.0 copy-start.1
  26.2 0.7 %copy-done.1 = f32[32,16,128]{2,1,0:T(8,128)} copy-done((f32[32,16,128]{2,1,0:T(8,128)}, f32[32,16,128]{2,1,0:T(8,128)S(1)}, u32[]{:S(2)}) %copy-start.1) | copy-done | bytes 262168
  26.9 6.0 %shard_map.96 = (f32[19,128,128]{2,1,0:T(8,128)}, f32[8,88,128]{2,1,0:T(8,128)}, f32[16,128]{1,0:T(8,128)}, f32[16,128]{1,0:T(8,128)}, f32[8,128]{1,0:T(8,128)}) custom-call(s32[3]{0:T(128)} %pad_add_fusion.refs_0_, f32[19,128,128]{2,1,0:T(8,128)} %bitcast.24, f32[128,128]{1,0:T(8,128)} %bitcast.27, s32[128,128]{1,0:T(8,128)} %bitcast.29, ...), custom_call_target="tpu_custom_call" | custom-call | tf_op jit(solution)/shard_map/pallas_call | solution.py:443
  32.9 11.0 %all_to_all.10.refs_2_ = f32[8,88,128]{2,1,0:T(8,128)S(1)} all-to-all(f32[8,88,128]{2,1,0:T(8,128)} %get-tuple-element.10), channel_id=1, replica_groups=mesh['gx'=4,'gy'=2,'gz'=4] {'gx','gy'}, dimensions={0} | all-to-all | bytes 720896 | tf_op jit(solution)/shard_map/all_to_all | solution.py:509
  43.9 0.0 copy-start
  43.9 0.7 %pad_maximum_fusion = f32[24,128]{1,0:T(8,128)S(1)} fusion(f32[8,128]{1,0:T(8,128)S(1)} %bitcast.33, f32[16,128]{1,0:T(8,128)} %get-tuple-element.11), kind=kLoop, calls=%fused_computation | loop fusion | flops 3072 | bytes 24576 | tf_op jit(solution)/shard_map/concatenate | solution.py:512
  44.7 2.1 %collective-permute-start = (f32[24,128]{1,0:T(8,128)S(1)}, f32[24,128]{1,0:T(8,128)S(1)}, u32[]{:S(2)}, u32[]{:S(2)}) collective-permute-start(f32[24,128]{1,0:T(8,128)S(1)} %pad_maximum_fusion), channel_id=1, source_target_pairs={{0,1},{1,2},{2,3},{4,5},{5,6},{6,7},{8,9},{9,10},{10,11},{12,13},{... | collective-permute-start | bytes 36872 | tf_op jit(solution)/shard_map/ppermute | solution.py:512
  46.8 0.7 %pad_maximum_fusion.1 = f32[24,128]{1,0:T(8,128)S(1)} fusion(f32[8,128]{1,0:T(8,128)S(1)} %bitcast.32, f32[16,128]{1,0:T(8,128)} %get-tuple-element.12), kind=kLoop, calls=%fused_computation.1 | loop fusion | flops 3072 | bytes 24576 | tf_op jit(solution)/shard_map/concatenate | solution.py:513
  47.5 1.3 %collective-permute-start.1 = (f32[24,128]{1,0:T(8,128)S(1)}, f32[24,128]{1,0:T(8,128)S(1)}, u32[]{:S(2)}, u32[]{:S(2)}) collective-permute-start(f32[24,128]{1,0:T(8,128)S(1)} %pad_maximum_fusion.1), channel_id=1, source_target_pairs={{1,0},{2,1},{3,2},{5,4},{6,5},{7,6},{9,8},{10,9},{11,10},{13,12},{... | collective-permute-start | bytes 36872 | tf_op jit(solution)/shard_map/ppermute | solution.py:513
  48.7 0.0 copy-done
  48.8 2.3 %shard_map.97.refs_6_ = f32[19,128,128]{2,1,0:T(8,128)} custom-call(s32[3]{0:T(128)} %pad_add_fusion.refs_0_, f32[19,128,128]{2,1,0:T(8,128)} %get-tuple-element.9.refs_1_, f32[8,88,128]{2,1,0:T(8,128)} %copy-done), custom_call_target="tpu_custom_call" | custom-call | tf_op jit(solution)/shard_map/pallas_call | solution.py:443
  51.0 0.0 collective-permute-done.refs_3_
  51.0 0.0 copy-start.2
  51.0 2.0 %collective-permute-done.1.refs_4_ = f32[24,128]{1,0:T(8,128)S(1)} collective-permute-done((f32[24,128]{1,0:T(8,128)S(1)}, f32[24,128]{1,0:T(8,128)S(1)}, u32[]{:S(2)}, u32[]{:S(2)}) %collective-permute-start.1) | collective-permute-done | bytes 12320 | tf_op jit(solution)/shard_map/ppermute | solution.py:513
  53.0 0.0 copy-start.3
  53.0 0.0 copy-done.2
  53.0 0.6 %copy-done.3 = f32[24,128]{1,0:T(8,128)} copy-done((f32[24,128]{1,0:T(8,128)}, f32[24,128]{1,0:T(8,128)S(1)}, u32[]{:S(2)}) %copy-start.3) | copy-done | bytes 12312
  53.6 3.2 %shard_map.98 = (f32[19,128,128]{2,1,0:T(8,128)}, f32[6,128]{1,0:T(8,128)}) custom-call(s32[3]{0:T(128)} %pad_add_fusion.refs_0_, f32[19,128,128]{2,1,0:T(8,128)} %get-tuple-element.9.refs_1_, f32[8,88,128]{2,1,0:T(8,128)} %copy-done, f32[24,128]{1,0:T(8,128)} %copy-done.2, f32[24,128]{1,0:T(8,128)} %copy-done.3, ...), custom_call_target="tpu_custom_call", output_to_operand_aliasing={{0}: (6, {})} | custom-call | tf_op jit(solution)/shard_map/pallas_call | solution.py:443
  56.9 1.3 %copy.17 = f32[1,1,1,6,128]{4,2,3,1,0:T(1,128)} copy(f32[1,1,1,6,128]{4,3,2,1,0:T(8,128)} %bitcast.34) | data formatting | bytes 6144
  (1 shorter events, 0.0 us)
Async XLA Ops:
  0.6 14.9 %copy-start.4 = (s32[1,1,1,12,128]{4,2,3,1,0:T(1,128)S(1)}, s32[1,1,1,12,128]{4,2,3,1,0:T(1,128)}, u32[]{:S(2)}) copy-start(s32[1,1,1,12,128]{4,2,3,1,0:T(1,128)} %param.13) | copy-start | bytes 18436
  8.2 18.1 %all-to-all-start = ((f32[32,16,128]{2,1,0:T(8,128)}), f32[32,16,128]{2,1,0:T(8,128)S(1)}, u32[]{:S(2)}, u32[]{:S(2)}) async-start(f32[32,16,128]{2,1,0:T(8,128)} %shard_map.95), calls=%async_computation | async-start | bytes 524288 | tf_op jit(solution)/shard_map/all_to_all | solution.py:491
  26.2 0.7 %copy-start.1 = (f32[32,16,128]{2,1,0:T(8,128)}, f32[32,16,128]{2,1,0:T(8,128)S(1)}, u32[]{:S(2)}) copy-start(f32[32,16,128]{2,1,0:T(8,128)S(1)} %all-to-all-done.refs_4_) | copy-start | bytes 786436
  43.9 4.8 %copy-start = (f32[8,88,128]{2,1,0:T(8,128)}, f32[8,88,128]{2,1,0:T(8,128)S(1)}, u32[]{:S(2)}) copy-start(f32[8,88,128]{2,1,0:T(8,128)S(1)} %all_to_all.10.refs_2_) | copy-start | bytes 1081348
  44.7 6.3 %collective-permute-start = (f32[24,128]{1,0:T(8,128)S(1)}, f32[24,128]{1,0:T(8,128)S(1)}, u32[]{:S(2)}, u32[]{:S(2)}) collective-permute-start(f32[24,128]{1,0:T(8,128)S(1)} %pad_maximum_fusion), channel_id=1, source_target_pairs={{0,1},{1,2},{2,3},{4,5},{5,6},{6,7},{8,9},{9,10},{10,11},{12,13},{... | collective-permute-start | bytes 36872 | tf_op jit(solution)/shard_map/ppermute | solution.py:512
  47.5 5.6 %collective-permute-start.1 = (f32[24,128]{1,0:T(8,128)S(1)}, f32[24,128]{1,0:T(8,128)S(1)}, u32[]{:S(2)}, u32[]{:S(2)}) collective-permute-start(f32[24,128]{1,0:T(8,128)S(1)} %pad_maximum_fusion.1), channel_id=1, source_target_pairs={{1,0},{2,1},{3,2},{5,4},{6,5},{7,6},{9,8},{10,9},{11,10},{13,12},{... | collective-permute-start | bytes 36872 | tf_op jit(solution)/shard_map/ppermute | solution.py:513
  51.0 2.0 %copy-start.2 = (f32[24,128]{1,0:T(8,128)}, f32[24,128]{1,0:T(8,128)S(1)}, u32[]{:S(2)}) copy-start(f32[24,128]{1,0:T(8,128)S(1)} %collective-permute-done.refs_3_) | copy-start | bytes 36868
  53.0 0.6 %copy-start.3 = (f32[24,128]{1,0:T(8,128)}, f32[24,128]{1,0:T(8,128)S(1)}, u32[]{:S(2)}) copy-start(f32[24,128]{1,0:T(8,128)S(1)} %collective-permute-done.1.refs_4_) | copy-start | bytes 36868

commit v3 on v2

--- a/solution.py
+++ b/solution.py
@@ -127,7 +127,7 @@
     total = lax.fori_loop(0, turns, step, jnp.zeros((16, touches), F32), unroll=2)
     sums = total[0:4] + total[4:8] + total[8:12]
     halves = touches // width
-    parts = [particles[...], touch[...].astype(F32)]
+    parts = [particles[i] for i in range(particles.shape[0])] + [touch[...].astype(F32)]
     for h in range(halves):
         parts.append(sums[:, h * width : (h + 1) * width])
     packet = jnp.concatenate(parts, axis=0)
@@ -402,7 +402,8 @@
         axis = 0 if o_x else 1
         keep = inside(axis, o_x + o_y)
         arrived = arrived + jnp.where(keep, got[neighbour(o_x, o_y), 0:8, :], 0.0)
-    particles[...] = arrived[0:6]
+    for i in range(particles.shape[0]):
+        particles[i] = arrived[i : i + 1]
 
     lane1 = lax.broadcasted_iota(jnp.int32, (1, cells), 1)
     fills = []
@@ -473,7 +474,7 @@
     pop = populations.reshape(19, cells, span_z)
     fraction = solid_fraction.reshape(cells, span_z)
     slots = intersection.reshape(cells, span_z)
-    records = particles.reshape(6, particle_slots)
+    records = particles.reshape(6, 1, particle_slots)
     touch_rows = touch.reshape(halves, span_z)
     rows = 6 + 5 * halves
     copies = call(
@@ -521,7 +522,7 @@
     )
     passed, arrived = call(
         bind(pass_kernel, span_x=span_x, span_y=span_y, mesh_shape=mesh_shape),
-        (shape_of(19, cells, span_z), shape_of(6, span_z)),
+        (shape_of(19, cells, span_z), shape_of(6, 1, span_z)),
         (HBM, VMEM),
         [
             pltpu.VMEM((cells, cells), F32),

time: 58.8 us -> 56.2 us (0.956)
  local copies, waits for them, and re-layouts: 4.43 us -> 1.9 us
    unnamed x13 -> x11, local copies, waits for them, and re-layouts: 4.42 us -> 1.89 us
  transfers between devices with their start and end apart: 3 -> 3, of which waited for: 2 -> 2; matrix products, arithmetic and copies ran while one was open for 3% -> 4% of each run, Pallas kernels for 4% -> 4%
where the time goes in v3:
time: 56.2 us; the launch traced here: 55.6 us
  Pallas kernels  17.7 us (31%)
  waiting for transfers between devices  11.5 us (20%)
  blocking collectives  11 us (20%)
  starting transfers between devices  10.7 us (19%)
  other arithmetic  2.11 us (4%)
  local copies, waits for them, and re-layouts  1.9 us (3%)
  between operations  0.73 us (1%)
    pallas_call x4, Pallas kernels, call(): pl.pallas_call(kernel, out_shape=outs, in_specs=specs, out_specs=out_spec...  17.7 us
    all_to_all x1, blocking collectives, body(): got = lax.all_to_all(send, ('gx', 'gy'), 0, 0)  11 us
    all_to_all x1, waiting for transfers between devices, body(): packets = lax.all_to_all(copies, axes, 0, 0)  9.47 us
    all_to_all x1, starting transfers between devices, body(): packets = lax.all_to_all(copies, axes, 0, 0)  7.33 us
    ppermute x1, starting transfers between devices, body(): z_below = lax.ppermute(jnp.concatenate([z_up, got[:, 6]]), 'gz', up)  2.06 us
    ppermute x1, waiting for transfers between devices, body(): z_above = lax.ppermute(jnp.concatenate([z_down, got[:, 7]]), 'gz', down)  2 us
    unnamed x11, local copies, waits for them, and re-layouts  1.89 us
    ppermute x1, starting transfers between devices, body(): z_above = lax.ppermute(jnp.concatenate([z_down, got[:, 7]]), 'gz', down)  1.28 us
  transfers between devices with their start and end apart: 3, of which 2 were waited for; matrix products, arithmetic and copies ran while one was open for 4% of the time, Pallas kernels for 4%

profile of v3, /device:TPU:0, one launch (start us, length us, event | category | flops | bytes accessed | tf_op | source)
XLA Modules:
  0.0 55.6 jit_solution(2691537401765760360)
XLA Ops:
  0.6 0.0 copy-start.4
  0.6 6.2 %shard_map.95 = f32[32,16,128]{2,1,0:T(8,128)} custom-call(f32[19,128,128]{2,1,0:T(8,128)} %bitcast.23, f32[128,128]{1,0:T(8,128)} %bitcast.26, s32[128,128]{1,0:T(8,128)} %bitcast.28, f32[6,1,128]{2,1,0:T(1,128)} %bitcast.35, s32[2,128]{1,0:T(2,128)} %bitcast.33), custom_call_target="tpu_custom_call" | custom-call | tf_op jit(solution)/shard_map/pallas_call | solution.py:444
  6.9 7.3 %all-to-all-start = ((f32[32,16,128]{2,1,0:T(8,128)}), f32[32,16,128]{2,1,0:T(8,128)S(1)}, u32[]{:S(2)}, u32[]{:S(2)}) async-start(f32[32,16,128]{2,1,0:T(8,128)} %shard_map.95), calls=%async_computation | async-start | bytes 524288 | tf_op jit(solution)/shard_map/all_to_all | solution.py:492
  14.2 0.0 copy-done.4
  14.2 0.6 %copy.22 = s32[1,1,1,12,128]{4,3,2,1,0:T(8,128)} copy(s32[1,1,1,12,128]{4,2,3,1,0:T(1,128)S(1)} %copy-done.4) | data formatting | bytes 12288
  14.8 0.7 %pad_add_fusion.refs_0_ = s32[3]{0:T(128)} fusion(s32[1]{0:T(128)} %bitcast.2, s32[1]{0:T(128)} %bitcast.1, s32[1]{0:T(128)} %bitcast), kind=kLoop, calls=%fused_computation.3 | loop fusion | flops 6 | bytes 24 | tf_op jit(solution)/shard_map/stack | solution.py:473
  15.5 9.5 %all-to-all-done.refs_4_ = f32[32,16,128]{2,1,0:T(8,128)S(1)} async-done(((f32[32,16,128]{2,1,0:T(8,128)}), f32[32,16,128]{2,1,0:T(8,128)S(1)}, u32[]{:S(2)}, u32[]{:S(2)}) %all-to-all-start) | async-done | bytes 262176 | tf_op jit(solution)/shard_map/all_to_all | solution.py:492
  25.0 0.0 copy-start.1
  25.0 0.7 %copy-done.1 = f32[32,16,128]{2,1,0:T(8,128)} copy-done((f32[32,16,128]{2,1,0:T(8,128)}, f32[32,16,128]{2,1,0:T(8,128)S(1)}, u32[]{:S(2)}) %copy-start.1) | copy-done | bytes 262168
  25.7 6.0 %shard_map.96 = (f32[19,128,128]{2,1,0:T(8,128)}, f32[8,88,128]{2,1,0:T(8,128)}, f32[16,128]{1,0:T(8,128)}, f32[16,128]{1,0:T(8,128)}, f32[8,128]{1,0:T(8,128)}) custom-call(s32[3]{0:T(128)} %pad_add_fusion.refs_0_, f32[19,128,128]{2,1,0:T(8,128)} %bitcast.24, f32[128,128]{1,0:T(8,128)} %bitcast.27, s32[128,128]{1,0:T(8,128)} %bitcast.29, ...), custom_call_target="tpu_custom_call" | custom-call | tf_op jit(solution)/shard_map/pallas_call | solution.py:444
  31.6 11.0 %all_to_all.10.refs_2_ = f32[8,88,128]{2,1,0:T(8,128)S(1)} all-to-all(f32[8,88,128]{2,1,0:T(8,128)} %get-tuple-element.10), channel_id=1, replica_groups=mesh['gx'=4,'gy'=2,'gz'=4] {'gx','gy'}, dimensions={0} | all-to-all | bytes 720896 | tf_op jit(solution)/shard_map/all_to_all | solution.py:510
  42.7 0.0 copy-start
  42.7 0.7 %pad_maximum_fusion = f32[24,128]{1,0:T(8,128)S(1)} fusion(f32[8,128]{1,0:T(8,128)S(1)} %bitcast.32, f32[16,128]{1,0:T(8,128)} %get-tuple-element.11), kind=kLoop, calls=%fused_computation | loop fusion | flops 3072 | bytes 24576 | tf_op jit(solution)/shard_map/concatenate | solution.py:513
  43.4 2.1 %collective-permute-start = (f32[24,128]{1,0:T(8,128)S(1)}, f32[24,128]{1,0:T(8,128)S(1)}, u32[]{:S(2)}, u32[]{:S(2)}) collective-permute-start(f32[24,128]{1,0:T(8,128)S(1)} %pad_maximum_fusion), channel_id=1, source_target_pairs={{0,1},{1,2},{2,3},{4,5},{5,6},{6,7},{8,9},{9,10},{10,11},{12,13},{... | collective-permute-start | bytes 36872 | tf_op jit(solution)/shard_map/ppermute | solution.py:513
  45.5 0.7 %pad_maximum_fusion.1 = f32[24,128]{1,0:T(8,128)S(1)} fusion(f32[8,128]{1,0:T(8,128)S(1)} %bitcast.31, f32[16,128]{1,0:T(8,128)} %get-tuple-element.12), kind=kLoop, calls=%fused_computation.1 | loop fusion | flops 3072 | bytes 24576 | tf_op jit(solution)/shard_map/concatenate | solution.py:514
  46.2 1.3 %collective-permute-start.1 = (f32[24,128]{1,0:T(8,128)S(1)}, f32[24,128]{1,0:T(8,128)S(1)}, u32[]{:S(2)}, u32[]{:S(2)}) collective-permute-start(f32[24,128]{1,0:T(8,128)S(1)} %pad_maximum_fusion.1), channel_id=1, source_target_pairs={{1,0},{2,1},{3,2},{5,4},{6,5},{7,6},{9,8},{10,9},{11,10},{13,12},{... | collective-permute-start | bytes 36872 | tf_op jit(solution)/shard_map/ppermute | solution.py:514
  47.5 0.0 copy-done
  47.5 2.3 %shard_map.97.refs_6_ = f32[19,128,128]{2,1,0:T(8,128)} custom-call(s32[3]{0:T(128)} %pad_add_fusion.refs_0_, f32[19,128,128]{2,1,0:T(8,128)} %get-tuple-element.9.refs_1_, f32[8,88,128]{2,1,0:T(8,128)} %copy-done), custom_call_target="tpu_custom_call" | custom-call | tf_op jit(solution)/shard_map/pallas_call | solution.py:444
  49.7 0.0 collective-permute-done.refs_3_
  49.8 0.0 copy-start.2
  49.8 2.0 %collective-permute-done.1.refs_4_ = f32[24,128]{1,0:T(8,128)S(1)} collective-permute-done((f32[24,128]{1,0:T(8,128)S(1)}, f32[24,128]{1,0:T(8,128)S(1)}, u32[]{:S(2)}, u32[]{:S(2)}) %collective-permute-start.1) | collective-permute-done | bytes 12320 | tf_op jit(solution)/shard_map/ppermute | solution.py:514
  51.8 0.0 copy-start.3
  51.8 0.0 copy-done.2
  51.8 0.6 %copy-done.3 = f32[24,128]{1,0:T(8,128)} copy-done((f32[24,128]{1,0:T(8,128)}, f32[24,128]{1,0:T(8,128)S(1)}, u32[]{:S(2)}) %copy-start.3) | copy-done | bytes 12312
  52.4 3.2 %shard_map.98 = (f32[19,128,128]{2,1,0:T(8,128)}, f32[6,1,128]{2,1,0:T(1,128)}) custom-call(s32[3]{0:T(128)} %pad_add_fusion.refs_0_, f32[19,128,128]{2,1,0:T(8,128)} %get-tuple-element.9.refs_1_, f32[8,88,128]{2,1,0:T(8,128)} %copy-done, f32[24,128]{1,0:T(8,128)} %copy-done.2, f32[24,128]{1,0:T(8,128)} %copy-done.3, ...), custom_call_target="tpu_custom_call", output_to_operand_aliasing={{0}: (6, {})} | custom-call | tf_op jit(solution)/shard_map/pallas_call | solution.py:444
  (1 shorter events, 0.0 us)
Async XLA Ops:
  0.6 13.6 %copy-start.4 = (s32[1,1,1,12,128]{4,2,3,1,0:T(1,128)S(1)}, s32[1,1,1,12,128]{4,2,3,1,0:T(1,128)}, u32[]{:S(2)}) copy-start(s32[1,1,1,12,128]{4,2,3,1,0:T(1,128)} %param.13) | copy-start | bytes 18436
  6.9 18.1 %all-to-all-start = ((f32[32,16,128]{2,1,0:T(8,128)}), f32[32,16,128]{2,1,0:T(8,128)S(1)}, u32[]{:S(2)}, u32[]{:S(2)}) async-start(f32[32,16,128]{2,1,0:T(8,128)} %shard_map.95), calls=%async_computation | async-start | bytes 524288 | tf_op jit(solution)/shard_map/all_to_all | solution.py:492
  25.0 0.7 %copy-start.1 = (f32[32,16,128]{2,1,0:T(8,128)}, f32[32,16,128]{2,1,0:T(8,128)S(1)}, u32[]{:S(2)}) copy-start(f32[32,16,128]{2,1,0:T(8,128)S(1)} %all-to-all-done.refs_4_) | copy-start | bytes 786436
  42.7 4.8 %copy-start = (f32[8,88,128]{2,1,0:T(8,128)}, f32[8,88,128]{2,1,0:T(8,128)S(1)}, u32[]{:S(2)}) copy-start(f32[8,88,128]{2,1,0:T(8,128)S(1)} %all_to_all.10.refs_2_) | copy-start | bytes 1081348
  43.4 6.3 %collective-permute-start = (f32[24,128]{1,0:T(8,128)S(1)}, f32[24,128]{1,0:T(8,128)S(1)}, u32[]{:S(2)}, u32[]{:S(2)}) collective-permute-start(f32[24,128]{1,0:T(8,128)S(1)} %pad_maximum_fusion), channel_id=1, source_target_pairs={{0,1},{1,2},{2,3},{4,5},{5,6},{6,7},{8,9},{9,10},{10,11},{12,13},{... | collective-permute-start | bytes 36872 | tf_op jit(solution)/shard_map/ppermute | solution.py:513
  46.2 5.6 %collective-permute-start.1 = (f32[24,128]{1,0:T(8,128)S(1)}, f32[24,128]{1,0:T(8,128)S(1)}, u32[]{:S(2)}, u32[]{:S(2)}) collective-permute-start(f32[24,128]{1,0:T(8,128)S(1)} %pad_maximum_fusion.1), channel_id=1, source_target_pairs={{1,0},{2,1},{3,2},{5,4},{6,5},{7,6},{9,8},{10,9},{11,10},{13,12},{... | collective-permute-start | bytes 36872 | tf_op jit(solution)/shard_map/ppermute | solution.py:514
  49.8 2.0 %copy-start.2 = (f32[24,128]{1,0:T(8,128)}, f32[24,128]{1,0:T(8,128)S(1)}, u32[]{:S(2)}) copy-start(f32[24,128]{1,0:T(8,128)S(1)} %collective-permute-done.refs_3_) | copy-start | bytes 36868
  51.8 0.6 %copy-start.3 = (f32[24,128]{1,0:T(8,128)}, f32[24,128]{1,0:T(8,128)S(1)}, u32[]{:S(2)}) copy-start(f32[24,128]{1,0:T(8,128)S(1)} %collective-permute-done.1.refs_4_) | copy-start | bytes 36868
